TPU v7x, 1024 devices: a whole 4x8x16 slice. The times are simulated.
1024 devices in a mesh: row: 32 (over z_hi, y), col: 32 (over x, z_lo, core).
Axes of the slice: x: 4, y: 8, z: 16 (z_hi: 4, z_lo: 4; z = z_hi * 4 + z_lo), core: 2. Of those that a mesh axis runs over, the one named last changes fastest.
Arguments:
- vectors: bfloat16 [65536, 32], P(('col', 'row')), may hold values from -6 to 6
- row_degree: float32 [65536], P('row'), may hold values from 1 to 16
- col_degree: float32 [65536], P('col'), may hold values from 1 to 16
- tiles: bfloat16 [32, 32, 16, 256, 256], P('row', 'col'), may hold values from 0 to 0.029907227
- tile_rows: int32 [32, 32, 16], P('row', 'col'), may hold values from 0 to 7
- tile_cols: int32 [32, 32, 16], P('row', 'col'), may hold values from 0 to 7
- tile_counts: int32 [32, 32], P('row', 'col'), may hold values from 1 to 16, as said below
- lent_tiles: bfloat16 [32, 32, 8, 256, 256], P('row', 'col'), may hold values from 0 to 0.029907227
- lent_rows: int32 [32, 32, 8], P('row', 'col'), may hold values from 0 to 7
- lent_cols: int32 [32, 32, 8], P('row', 'col'), may hold values from 0 to 7
- lent_counts: int32 [32, 32], P('row', 'col'), may hold values from 0 to 8, as said below
Outputs:
- first: float32 [65536, 32], P(('row', 'col'))
- second: float32 [65536, 32], P(('col', 'row'))
Inputs may be any that keep to these rules, and one draw needn't show every extreme that they name: `tile_counts`: in every tile-row block at least one block uses all 16 own slots; most use far fewer. `lent_counts`: in every tile-row block exactly one device holds 8 used borrowed slots: it is the partner (column XOR 16) of one block of that row that uses all 16 own slots (other blocks of the row may also use 16); all other counts are 0.
All inputs are finite; a program needn't handle non-finite values.
Results may differ from a plain program's by a relative error of at most 0.0033.
Values may be sent and summed in bfloat16 or wider, within the bound.
No kernel may reach another device: no remote copies, remote signals or barrier semaphores. Data moves between devices by JAX's collectives and lax.ppermute only.
A program may use at most 32 MiB of HBM per device.

v0:
```python
import jax
import jax.numpy as jnp
from jax import lax
from jax.sharding import PartitionSpec as P


def partner(block, axis, distance):
    count = lax.axis_size(axis)
    route = []
    for low in range(count):
        high = low | 1 << distance
        if high != low and high < count:
            route += [(low, high), (high, low)]
    return lax.ppermute(block, axis, route)


def apply_tiles(block_tiles, in_index, out_index, live, source, out_tiles, flip):
    count_slots, tile = (block_tiles.shape[0], block_tiles.shape[1])
    width = source.shape[1]
    in_tiles = source.shape[0] // tile
    pick = (in_index[:, None] == jnp.arange(in_tiles, dtype=jnp.int32)[None, :]).astype(
        jnp.bfloat16
    )
    picked = jnp.dot(
        pick, source.reshape(in_tiles, tile * width), preferred_element_type=jnp.float32
    )
    picked = picked.astype(jnp.bfloat16).reshape(count_slots, tile, width)
    if flip:
        prod = jnp.einsum("sab,sak->sbk", block_tiles, picked, preferred_element_type=jnp.float32)
    else:
        prod = jnp.einsum("sab,sbk->sak", block_tiles, picked, preferred_element_type=jnp.float32)
    place = (
        (out_index[None, :] == jnp.arange(out_tiles, dtype=jnp.int32)[:, None]) & live[None, :]
    ).astype(jnp.float32)
    total = jnp.dot(
        place,
        prod.reshape(count_slots, tile * width),
        precision=lax.Precision.HIGHEST,
        preferred_element_type=jnp.float32,
    )
    return total.reshape(out_tiles * tile, width)


def shards(
    vectors,
    row_degree,
    col_degree,
    tiles,
    tile_rows,
    tile_cols,
    tile_counts,
    lent_tiles,
    lent_rows,
    lent_cols,
    lent_counts,
):
    block_tiles = tiles.reshape(tiles.shape[2:])
    borrowed = lent_tiles.reshape(lent_tiles.shape[2:])
    tile = block_tiles.shape[1]
    slot_rows = tile_rows.reshape(-1)
    slot_cols = tile_cols.reshape(-1)
    borrow_rows = lent_rows.reshape(-1)
    borrow_cols = lent_cols.reshape(-1)
    used = tile_counts.reshape(())
    borrow_used = lent_counts.reshape(())
    live = jnp.arange(block_tiles.shape[0], dtype=jnp.int32) < used
    borrow_live = jnp.arange(borrowed.shape[0], dtype=jnp.int32) < borrow_used
    pair_bit = lax.axis_size("col").bit_length() - 2
    row_place = lax.axis_index("row")
    col_place = lax.axis_index("col")
    shard = vectors.shape[0]
    row_count = row_degree.shape[0] // tile
    col_count = col_degree.shape[0] // tile
    col_scale = lax.rsqrt(lax.dynamic_slice_in_dim(col_degree, row_place * shard, shard, 0))
    scaled = (vectors.astype(jnp.float32) * col_scale[:, None]).astype(jnp.bfloat16)
    column_block = lax.all_gather(scaled, "row", axis=0, tiled=True)
    partial_value = apply_tiles(
        block_tiles, slot_cols, slot_rows, live, column_block, row_count, False
    )
    packed = jnp.stack([borrow_rows, borrow_cols, borrow_live.astype(jnp.int32)])
    home_tiles, home_index = partner((borrowed, packed), "col", pair_bit)
    home_live = home_index[2] > 0
    partial_value = partial_value + apply_tiles(
        home_tiles, home_index[1], home_index[0], home_live, column_block, row_count, False
    )
    row_scale = lax.rsqrt(row_degree)
    own = lax.psum_scatter(partial_value, "col", scatter_dimension=0, tiled=True)
    first = own * lax.dynamic_slice_in_dim(row_scale, col_place * shard, shard, 0)[:, None]
    row_block = lax.all_gather(first.astype(jnp.bfloat16), "col", axis=0, tiled=True)
    partial_back = apply_tiles(block_tiles, slot_rows, slot_cols, live, row_block, col_count, True)
    partial_back = partial_back + apply_tiles(
        home_tiles, home_index[0], home_index[1], home_live, row_block, col_count, True
    )
    second = (
        lax.psum_scatter(partial_back, "row", scatter_dimension=0, tiled=True) * col_scale[:, None]
    )
    return (first, second)


def solution(mesh):
    return jax.shard_map(
        shards,
        mesh=mesh,
        in_specs=(
            P(("col", "row"), None),
            P("row"),
            P("col"),
            P("row", "col", None, None, None),
            P("row", "col", None),
            P("row", "col", None),
            P("row", "col"),
            P("row", "col", None, None, None),
            P("row", "col", None),
            P("row", "col", None),
            P("row", "col"),
        ),
        out_specs=(P(("row", "col"), None), P(("col", "row"), None)),
        check_vma=False,
    )
```

profile of v0, /device:TPU:2, one launch (start us, length us, event | category | flops | bytes accessed | tf_op | source)
XLA Modules:
  0.0 605.9 jit_solution(8123457673104643586)
XLA Ops:
  8.7 4.0 collective-permute-start
  12.7 3.3 collective-permute-start.1
  17.8 110.3 %all-gather = bf16[32,64,32]{1,2,0:T(8,128)(2,1)S(1)} all-gather(bf16[1,64,32]{1,2,0:T(8,128)(2,1)S(1)} %copy.31), channel_id=1, replica_groups=mesh['row'=32,'col'=32] {'row'}, dimensions={0}, use_global_device_ids=true | all-gather | bytes 135168 | tf_op jit(solution)/shard_map/all_gather | solution.py:76
  128.9 0.9 convolution_convert_fusion.1
  129.8 0.8 reshape.78
  130.6 1.5 fusion.4
  132.2 3.0 copy.34
  135.2 2.5 reshape.80
  138.4 1.0 fusion.14
  141.5 1.6 convolution_bitcast_fusion.1
  144.0 1.2 convolution_add_fusion.1
  145.2 1.3 add.24
  147.3 124.0 %reduce-scatter.3.cloned.1.call-done = f32[64,32]{1,0:T(8,128)} async-done(((f32[2048,32]{1,0:T(8,128)}), f32[64,32]{1,0:T(8,128)}) %reduce-scatter.3.cloned.1.call-update) | async-done | bytes 8208 | tf_op jit(solution)/shard_map/reduce_scatter | solution.py:87
  271.3 1.4 convert_bitcast_fusion
  272.8 51.5 %all-gather.1 = bf16[32,64,32]{1,2,0:T(8,128)(2,1)S(1)} all-gather(bf16[1,64,32]{1,2,0:T(8,128)(2,1)S(1)} %copy.37), channel_id=1, replica_groups=mesh['row'=32,'col'=32] {'col'}, dimensions={0}, use_global_device_ids=true | all-gather | bytes 135168 | tf_op jit(solution)/shard_map/all_gather | solution.py:89
  326.5 1.3 fusion.7
  327.7 3.0 copy.40
  330.7 2.5 reshape.87
  333.3 1.0 fusion.19
  334.7 1.5 convolution_bitcast_fusion
  337.1 1.2 convolution_add_fusion
  338.3 1.3 add.27
  340.3 257.3 %reduce-scatter.5.cloned.1.call-done = f32[64,32]{1,0:T(8,128)} async-done(((f32[2048,32]{1,0:T(8,128)}), f32[64,32]{1,0:T(8,128)}) %reduce-scatter.5.cloned.1.call-update) | async-done | bytes 8208 | tf_op jit(solution)/shard_map/reduce_scatter | solution.py:95
  597.6 0.8 broadcast_multiply_fusion.1
  (45 shorter events, 11.8 us)
Async XLA Ops:
  7.2 123.5 %copy-start = (bf16[1,1,16,256,256]{4,3,2,1,0:T(8,128)(2,1)S(1)}, bf16[1,1,16,256,256]{4,3,2,1,0:T(8,128)(2,1)}, u32[]{:S(2)}) copy-start(bf16[1,1,16,256,256]{4,3,2,1,0:T(8,128)(2,1)} %param.14) | copy-start | bytes 6291460
  7.2 264.1 %reduce-scatter.3.cloned.1.call-start = ((), (), s32[]{:S(2)}) async-start(), calls=%async_computation.2 | async-start | bytes 1081344 | tf_op jit(solution)/shard_map/reduce_scatter | solution.py:87
  8.7 130.7 %collective-permute-start = (s32[3,8]{1,0:T(4,128)S(1)}, s32[3,8]{1,0:T(4,128)}, u32[]{:S(2)}, u32[]{:S(2)}) collective-permute-start(s32[3,8]{1,0:T(4,128)S(1)} %pad_add_fusion), channel_id=1, source_target_pairs={{0,16},{16,0},{1,17},{17,1},{2,18},{18,2},{3,19},{19,3},{4,20},{20... | collective-permute-start | bytes 296 | tf_op jit(solution)/shard_map/ppermute | solution.py:14
  12.7 128.7 %collective-permute-start.1 = (bf16[8,256,256]{2,1,0:T(8,128)(2,1)}, bf16[8,256,256]{2,1,0:T(8,128)(2,1)}, u32[]{:S(2)}, u32[]{:S(2)}) collective-permute-start(bf16[8,256,256]{2,1,0:T(8,128)(2,1)} %bitcast.56), channel_id=1, source_target_pairs={{0,16},{16,0},{1,17},{17,1},{2,18},{18,2},{3,19},{19,3},{4,20},{20... | collective-permute-start | bytes 3145736 | tf_op jit(solution)/shard_map/ppermute | solution.py:14
  132.2 6.2 %copy-start.2 = (s32[1,1,16]{2,1,0:T(1,128)S(1)}, s32[1,1,16]{2,1,0:T(1,128)}, u32[]{:S(2)}) copy-start(s32[1,1,16]{2,1,0:T(1,128)} %param.15) | copy-start | bytes 196
  141.5 2.5 copy-start.4
  146.5 451.1 %reduce-scatter.5.cloned.1.call-start = ((), (), s32[]{:S(2)}) async-start(), calls=%async_computation.3 | async-start | bytes 1081344 | tf_op jit(solution)/shard_map/reduce_scatter | solution.py:95
  327.7 5.5 copy-start.3
  334.7 2.4 copy-start.5
  336.5 3.1 copy-start.1
Sparse Core Ops, SparseCore 0:
  146.6 124.6 reduce-scatter.2
  339.7 257.8 reduce-scatter.4
where the time goes:
time: 607 us; the launch traced here: 606 us
  waiting for transfers between devices  381 us (63%)
  blocking collectives  162 us (27%)
  local copies, waits for them, and re-layouts  24 us (4%)
  between operations  15.7 us (3%)
  matrix products  12 us (2%)
  starting transfers between devices  7.42 us (1%)
    reduce_scatter x1, waiting for transfers between devices, shards(): lax.psum_scatter(partial_back, 'row', scatter_dimension=0, tiled=True)  257 us
    reduce_scatter x1, waiting for transfers between devices, shards(): lax.psum_scatter(partial_value, 'col', scatter_dimension=0, tiled=True)  124 us
    all_gather x1, blocking collectives, shards(): column_block = lax.all_gather(scaled, 'row', axis=0, tiled=True)  110 us
    all_gather x1, blocking collectives, shards(): lax.all_gather(first.astype(jnp.bfloat16), 'col', axis=0, tiled=True)  51.5 us
  transfers between devices with their start and end apart: 4, of which 2 were waited for; matrix products, arithmetic and copies ran while one was open for 3% of the time, Pallas kernels for 0%

commit v1 on v0

v1 whole, which is shorter than its diff:
```python
import jax
import jax.numpy as jnp
from jax import lax
from jax.experimental import pallas as pl
from jax.experimental.pallas import tpu as pltpu
from jax.sharding import PartitionSpec as P

GROUP = 4
F32 = jnp.float32
BF16 = jnp.bfloat16


def vmem():
    return pl.BlockSpec(memory_space=pltpu.VMEM)


def smem():
    return pl.BlockSpec(memory_space=pltpu.SMEM)


def any_space():
    return pl.BlockSpec(memory_space=pl.ANY)


def low_lanes(shape):
    return lax.broadcasted_iota(jnp.int32, shape, len(shape) - 1) < shape[-1] // 2


def shard_scale(degree_ref, place):
    line = degree_ref[pl.ds(place // 2, 1), :]
    turned = pltpu.roll(line, 64, 1)
    first_half = place % 2 == 0
    low = low_lanes(line.shape)
    both = jnp.where(low == first_half, line, turned)
    return lax.rsqrt(both)


def pack_kernel(place_ref, vectors_ref, degree_ref, out_ref):
    scale = shard_scale(degree_ref, place_ref[0])
    values = vectors_ref[...].astype(F32)
    half = values.shape[0] // 2
    wide = jnp.concatenate([values[:half], values[half:]], axis=1) * scale
    packed = wide.astype(BF16)
    for copy in range(out_ref.shape[0]):
        out_ref[copy] = packed


def unpack_source(source_ref, wide_ref):
    low = low_lanes((16, 128))
    for pair in range(source_ref.shape[0] // 2):
        even = source_ref[2 * pair].astype(F32)
        odd = source_ref[2 * pair + 1].astype(F32)
        top = jnp.where(low, even, pltpu.roll(odd, 64, 1))
        bottom = jnp.where(low, pltpu.roll(even, 64, 1), odd)
        lanes = slice(128 * (pair % 2), 128 * (pair % 2) + 128)
        wide_ref[pair // 2, 0:16, lanes] = top.astype(BF16)
        wide_ref[pair // 2, 16:32, lanes] = bottom.astype(BF16)


def pack_total(total_ref, out_ref):
    low = low_lanes((16, 128))
    for pair in range(out_ref.shape[0] // 2):
        lanes = slice(128 * (pair % 2), 128 * (pair % 2) + 128)
        top = total_ref[pair // 2, 0:16, lanes]
        bottom = total_ref[pair // 2, 16:32, lanes]
        even = jnp.where(low, top, pltpu.roll(bottom, 64, 1))
        odd = jnp.where(low, pltpu.roll(top, 64, 1), bottom)
        out_ref[2 * pair] = even.astype(out_ref.dtype)
        out_ref[2 * pair + 1] = odd.astype(out_ref.dtype)


def tile_copy(tiles_ref, buffer_ref, sems, slot):
    return pltpu.make_async_copy(tiles_ref.at[slot], buffer_ref.at[slot], sems.at[slot])


def start_tiles(tiles_ref, buffer_ref, sems, groups):
    def start(slot, carry):
        tile_copy(tiles_ref, buffer_ref, sems, slot).start()
        return carry

    lax.fori_loop(0, groups * GROUP, start, 0)


def add_tiles(table_ref, at_in, at_out, used, groups, wide_ref, total_ref, tiles_ref, buffer_ref, sems, flip):
    contract = (((1,), (0,)), ((), ())) if flip else (((1,), (1,)), ((), ()))

    def body(group, carry):
        base = group * GROUP
        prods = []
        for lane in range(GROUP):
            slot = base + lane
            tile_copy(tiles_ref, buffer_ref, sems, slot).wait()
            source = wide_ref[table_ref[at_in + slot]]
            prod = lax.dot_general(
                source, buffer_ref[slot], contract, preferred_element_type=F32
            )
            prods.append(jnp.where(slot < used, prod, 0.0))
        for lane in range(GROUP):
            spot = table_ref[at_out + base + lane]
            total_ref[spot] = total_ref[spot] + prods[lane]
        return carry

    lax.fori_loop(0, groups, body, 0)


def product_kernel(at_in, at_out, at_used, flip, packed, seeded):
    def kernel(*refs):
        if seeded:
            table_ref, source_ref, tiles_ref, seed_ref, out_ref = refs[:5]
        else:
            table_ref, source_ref, tiles_ref, out_ref = refs[:4]
        wide_ref, total_scratch, buffer_ref, sems = refs[-4:]
        used = table_ref[at_used]
        groups = (used + GROUP - 1) // GROUP
        start_tiles(tiles_ref, buffer_ref, sems, groups)
        total_ref = total_scratch if packed else out_ref
        if seeded:
            total_ref[...] = seed_ref[...]
        else:
            total_ref[...] = jnp.zeros_like(total_ref)

        @pl.when(used > 0)
        def _():
            unpack_source(source_ref, wide_ref)

        add_tiles(
            table_ref, at_in, at_out, used, groups, wide_ref, total_ref, tiles_ref, buffer_ref, sems, flip
        )
        if packed:
            pack_total(total_ref, out_ref)

    return kernel


def product(table, source, tiles, at_in, at_out, at_used, flip, out_dtype=None, seed=None):
    slots = tiles.shape[0]
    chunks = source.shape[0]
    wide = (chunks // 4, 32, 256)
    packed = out_dtype is not None
    out = (
        jax.ShapeDtypeStruct((chunks, 16, 128), out_dtype)
        if packed
        else jax.ShapeDtypeStruct(wide, F32)
    )
    seeds = [] if seed is None else [seed]
    return pl.pallas_call(
        product_kernel(at_in, at_out, at_used, flip, packed, seed is not None),
        out_shape=out,
        in_specs=[smem(), vmem(), any_space()] + [vmem()] * len(seeds),
        out_specs=vmem(),
        scratch_shapes=[
            pltpu.VMEM(wide, BF16),
            pltpu.VMEM(wide if packed else (1, 8, 128), F32),
            pltpu.VMEM(tiles.shape, tiles.dtype),
            pltpu.SemaphoreType.DMA((slots,)),
        ],
    )(table, source, tiles, *seeds)


def sum_chunks(received_ref):
    parts = [received_ref[chunk].astype(F32) for chunk in range(received_ref.shape[0])]
    while len(parts) > 1:
        parts = [parts[k] + parts[k + 1] for k in range(0, len(parts), 2)]
    return parts[0]


def store_shard(out_ref, wide):
    out_ref[0:16, :] = wide[:, 0:64]
    out_ref[16:32, :] = pltpu.roll(wide, 64, 1)[:, 0:64]


def middle_kernel(place_ref, received_ref, degree_ref, out_ref, copies_ref):
    wide = sum_chunks(received_ref) * shard_scale(degree_ref, place_ref[1])
    store_shard(out_ref, wide)
    packed = wide.astype(BF16)
    for copy in range(copies_ref.shape[0]):
        copies_ref[copy] = packed


def last_kernel(place_ref, received_ref, degree_ref, out_ref):
    wide = sum_chunks(received_ref) * shard_scale(degree_ref, place_ref[0])
    store_shard(out_ref, wide)


def exchange(chunks, axis):
    return lax.all_to_all(chunks, axis, 0, 0, tiled=True)


def partner(block):
    count = lax.axis_size("col")
    return lax.ppermute(block, "col", [(k, k ^ (count // 2)) for k in range(count)])


def shards(
    vectors,
    row_degree,
    col_degree,
    tiles,
    tile_rows,
    tile_cols,
    tile_counts,
    lent_tiles,
    lent_rows,
    lent_cols,
    lent_counts,
):
    own = tiles.reshape(tiles.shape[2:])
    lent = lent_tiles.reshape(lent_tiles.shape[2:])
    slots, lents = own.shape[0], lent.shape[0]
    table = jnp.concatenate(
        [
            tile_rows.reshape(-1),
            tile_cols.reshape(-1),
            lent_rows.reshape(-1),
            lent_cols.reshape(-1),
            tile_counts.reshape(-1),
            lent_counts.reshape(-1),
        ]
    )
    at_rows, at_cols = 0, slots
    at_lent_rows, at_lent_cols = 2 * slots, 2 * slots + lents
    at_used, at_lent_used = 2 * slots + 2 * lents, 2 * slots + 2 * lents + 1
    place = jnp.stack([lax.axis_index("row"), lax.axis_index("col")]).astype(jnp.int32)
    row_lines = row_degree.reshape(-1, 128)
    col_lines = col_degree.reshape(-1, 128)
    row_size, col_size = lax.axis_size("row"), lax.axis_size("col")

    copies = pl.pallas_call(
        pack_kernel,
        out_shape=jax.ShapeDtypeStruct((row_size, 16, 128), BF16),
        in_specs=[smem(), vmem(), vmem()],
        out_specs=vmem(),
    )(place, vectors.T, col_lines)
    source = exchange(copies, "row")
    lent_source = partner(source)
    total = product(table, source, own, at_cols, at_rows, at_used, False)
    partial_value = product(
        table, lent_source, lent, at_lent_cols, at_lent_rows, at_lent_used, False, BF16, total
    )
    first, middle_copies = pl.pallas_call(
        middle_kernel,
        out_shape=(
            jax.ShapeDtypeStruct((32, 64), F32),
            jax.ShapeDtypeStruct((col_size, 16, 128), BF16),
        ),
        in_specs=[smem(), vmem(), vmem()],
        out_specs=(vmem(), vmem()),
    )(place, exchange(partial_value, "col"), row_lines)
    middle = exchange(middle_copies, "col")
    lent_back = product(
        table, middle, lent, at_lent_rows, at_lent_cols, at_lent_used, True, BF16
    )
    home_back = partner(lent_back)
    own_back = product(table, middle, own, at_rows, at_cols, at_used, True, F32)
    partial_back = (own_back + home_back.astype(F32)).astype(BF16)
    second = pl.pallas_call(
        last_kernel,
        out_shape=jax.ShapeDtypeStruct((32, 64), F32),
        in_specs=[smem(), vmem(), vmem()],
        out_specs=vmem(),
    )(place, exchange(partial_back, "row"), col_lines)
    return (first.T, second.T)


def solution(mesh):
    return jax.shard_map(
        shards,
        mesh=mesh,
        in_specs=(
            P(("col", "row"), None),
            P("row"),
            P("col"),
            P("row", "col", None, None, None),
            P("row", "col", None),
            P("row", "col", None),
            P("row", "col"),
            P("row", "col", None, None, None),
            P("row", "col", None),
            P("row", "col", None),
            P("row", "col"),
        ),
        out_specs=(P(("row", "col"), None), P(("col", "row"), None)),
        check_vma=False,
    )
```

time: 607 us -> 128 us (0.21)
  the two profiles are of different devices: /device:TPU:2 before, /device:TPU:8 now
where the time goes in v1:
time: 128 us
  blocking collectives  92.1 us (72%)
  Pallas kernels  19.5 us (15%)
  starting transfers between devices  10.3 us (8%)
  local copies, waits for them, and re-layouts  2.03 us (2%)
  between operations  2.01 us (2%)
  other arithmetic  1.63 us (1%)
    all_to_all x4, blocking collectives, exchange(): return lax.all_to_all(chunks, axis, 0, 0, tiled=True)  92.1 us
    pallas_call x4, Pallas kernels, product(): pl.pallas_call(product_kernel(at_in, at_out, at_used, flip, packed, seed...  14.7 us
    ppermute x2, starting transfers between devices, partner(): lax.ppermute(block, 'col', [(k, k ^ count // 2) for k in range(count)])  10.3 us
  transfers between devices with their start and end apart: 2, of which 0 were waited for; matrix products, arithmetic and copies ran while one was open for 1% of the time, Pallas kernels for 9%

profile of v1, /device:TPU:8, one launch (start us, length us, event | category | flops | bytes accessed | tf_op | source)
XLA Modules:
  0.0 127.5 jit_solution(10784034279062326065)
XLA Ops:
  0.6 0.7 pad_add_fusion.place_ref
  1.3 1.5 %shard_map.122 = bf16[32,16,128]{2,1,0:T(8,128)(2,1)} custom-call(s32[2]{0:T(128)} %pad_add_fusion.place_ref, bf16[32,64]{1,0:T(8,128)(2,1)} %bitcast.24, f32[16,128]{1,0:T(8,128)} %bitcast.21), custom_call_target="tpu_custom_call" | custom-call | tf_op jit(solution)/shard_map/pallas_call | solution.py:228
  2.8 43.6 %all_to_all.20.refs_1_ = bf16[32,16,128]{2,1,0:T(8,128)(2,1)S(1)} all-to-all(bf16[32,16,128]{2,1,0:T(8,128)(2,1)} %shard_map.122), channel_id=1, replica_groups=mesh['row'=32,'col'=32] {'row'}, dimensions={0} | all-to-all | bytes 262144 | tf_op jit(solution)/shard_map/all_to_all | solution.py:186
  46.4 0.0 copy-start
  46.4 4.9 %collective-permute-start = (bf16[32,16,128]{2,1,0:T(8,128)(2,1)S(1)}, bf16[32,16,128]{2,1,0:T(8,128)(2,1)S(1)}, u32[]{:S(2)}, u32[]{:S(2)}) collective-permute-start(bf16[32,16,128]{2,1,0:T(8,128)(2,1)S(1)} %all_to_all.20.refs_1_), channel_id=1, source_target_pairs={{0,16},{1,17},{2,18},{3,19},{4,20},{5,21},{6,22},{7,23},{8,24},{9,... | collective-permute-start | bytes 393224 | tf_op jit(solution)/shard_map/ppermute | solution.py:191
  52.6 1.4 %concatenate.3.refs_0_ = s32[50]{0:T(128)} concatenate(s32[16]{0:T(128)} %bitcast.26, s32[16]{0:T(128)} %bitcast.27, s32[8]{0:T(128)} %bitcast.28, s32[8]{0:T(128)} %bitcast.29, s32[1]{0:T(128)} %bitcast.15, s32[1]{0:T(128)} %bitcast.16), dimensions={0} | concatenate | bytes 400 | tf_op jit(solution)/shard_map/concatenate | solution.py:210
  54.0 0.0 copy-done
  54.0 5.7 %shard_map.123.refs_3_ = f32[8,32,256]{2,1,0:T(8,128)} custom-call(s32[50]{0:T(128)} %concatenate.3.refs_0_, bf16[32,16,128]{2,1,0:T(8,128)(2,1)} %copy-done, bf16[16,256,256]{2,1,0:T(8,128)(2,1)} %bitcast.17), custom_call_target="tpu_custom_call" | custom-call | tf_op jit(solution)/shard_map/pallas_call | solution.py:146
  59.7 0.0 collective-permute-done.refs_1_
  59.7 0.0 copy-start.1
  59.7 0.7 copy-done.1
  60.3 1.9 %shard_map.124 = bf16[32,16,128]{2,1,0:T(8,128)(2,1)} custom-call(s32[50]{0:T(128)} %concatenate.3.refs_0_, bf16[32,16,128]{2,1,0:T(8,128)(2,1)} %copy-done.1, bf16[8,256,256]{2,1,0:T(8,128)(2,1)} %bitcast.19, f32[8,32,256]{2,1,0:T(8,128)} %shard_map.123.refs_3_), custom_call_target="tpu_custom_call" | custom-call | tf_op jit(solution)/shard_map/pallas_call | solution.py:146
  62.2 13.4 %all_to_all.21.received_ref = bf16[32,16,128]{2,1,0:T(8,128)(2,1)} all-to-all(bf16[32,16,128]{2,1,0:T(8,128)(2,1)} %shard_map.124), channel_id=1, replica_groups=mesh['row'=32,'col'=32] {'col'}, dimensions={0} | all-to-all | bytes 262144 | tf_op jit(solution)/shard_map/all_to_all | solution.py:186
  75.6 1.7 %shard_map.125 = (f32[32,64]{1,0:T(8,128)}, bf16[32,16,128]{2,1,0:T(8,128)(2,1)}) custom-call(s32[2]{0:T(128)} %pad_add_fusion.place_ref, bf16[32,16,128]{2,1,0:T(8,128)(2,1)} %all_to_all.21.received_ref, f32[16,128]{1,0:T(8,128)} %bitcast.25), custom_call_target="tpu_custom_call" | custom-call | tf_op jit(solution)/shard_map/pallas_call | solution.py:240
  77.3 13.4 %all_to_all.22.refs_1_ = bf16[32,16,128]{2,1,0:T(8,128)(2,1)} all-to-all(bf16[32,16,128]{2,1,0:T(8,128)(2,1)} %get-tuple-element.5), channel_id=1, replica_groups=mesh['row'=32,'col'=32] {'col'}, dimensions={0} | all-to-all | bytes 262144 | tf_op jit(solution)/shard_map/all_to_all | solution.py:186
  90.7 1.8 %shard_map.127 = bf16[32,16,128]{2,1,0:T(8,128)(2,1)} custom-call(s32[50]{0:T(128)} %concatenate.3.refs_0_, bf16[32,16,128]{2,1,0:T(8,128)(2,1)} %all_to_all.22.refs_1_, bf16[8,256,256]{2,1,0:T(8,128)(2,1)} %bitcast.20), custom_call_target="tpu_custom_call" | custom-call | tf_op jit(solution)/shard_map/pallas_call | solution.py:146
  92.5 5.4 %collective-permute-start.1 = (bf16[32,16,128]{2,1,0:T(8,128)(2,1)}, bf16[32,16,128]{2,1,0:T(8,128)(2,1)S(1)}, u32[]{:S(2)}, u32[]{:S(2)}) collective-permute-start(bf16[32,16,128]{2,1,0:T(8,128)(2,1)} %shard_map.127), channel_id=1, source_target_pairs={{0,16},{1,17},{2,18},{3,19},{4,20},{5,21},{6,22},{7,23},{8,24},{9,... | collective-permute-start | bytes 393224 | tf_op jit(solution)/shard_map/ppermute | solution.py:191
  97.9 5.3 %shard_map.126 = f32[32,16,128]{2,1,0:T(8,128)} custom-call(s32[50]{0:T(128)} %concatenate.3.refs_0_, bf16[32,16,128]{2,1,0:T(8,128)(2,1)} %all_to_all.22.refs_1_, bf16[16,256,256]{2,1,0:T(8,128)(2,1)} %bitcast.18), custom_call_target="tpu_custom_call" | custom-call | tf_op jit(solution)/shard_map/pallas_call | solution.py:146
  103.2 0.0 collective-permute-done.1
  103.2 1.0 add_convert_fusion
  104.2 21.7 %all_to_all.23.received_ref = bf16[32,16,128]{2,1,0:T(8,128)(2,1)} all-to-all(bf16[32,16,128]{2,1,0:T(8,128)(2,1)S(1)} %add_convert_fusion), channel_id=1, replica_groups=mesh['row'=32,'col'=32] {'row'}, dimensions={0} | all-to-all | bytes 262144 | tf_op jit(solution)/shard_map/all_to_all | solution.py:186
  125.9 1.7 %shard_map.128 = f32[32,64]{1,0:T(8,128)} custom-call(s32[2]{0:T(128)} %pad_add_fusion.place_ref, bf16[32,16,128]{2,1,0:T(8,128)(2,1)} %all_to_all.23.received_ref, f32[16,128]{1,0:T(8,128)} %bitcast.22), custom_call_target="tpu_custom_call" | custom-call | tf_op jit(solution)/shard_map/pallas_call | solution.py:256
Async XLA Ops:
  46.4 7.6 %copy-start = (bf16[32,16,128]{2,1,0:T(8,128)(2,1)}, bf16[32,16,128]{2,1,0:T(8,128)(2,1)S(1)}, u32[]{:S(2)}) copy-start(bf16[32,16,128]{2,1,0:T(8,128)(2,1)S(1)} %all_to_all.20.refs_1_) | copy-start | bytes 393220
  46.4 13.3 %collective-permute-start = (bf16[32,16,128]{2,1,0:T(8,128)(2,1)S(1)}, bf16[32,16,128]{2,1,0:T(8,128)(2,1)S(1)}, u32[]{:S(2)}, u32[]{:S(2)}) collective-permute-start(bf16[32,16,128]{2,1,0:T(8,128)(2,1)S(1)} %all_to_all.20.refs_1_), channel_id=1, source_target_pairs={{0,16},{1,17},{2,18},{3,19},{4,20},{5,21},{6,22},{7,23},{8,24},{9,... | collective-permute-start | bytes 393224 | tf_op jit(solution)/shard_map/ppermute | solution.py:191
  59.7 0.7 copy-start.1
  92.5 10.7 %collective-permute-start.1 = (bf16[32,16,128]{2,1,0:T(8,128)(2,1)}, bf16[32,16,128]{2,1,0:T(8,128)(2,1)S(1)}, u32[]{:S(2)}, u32[]{:S(2)}) collective-permute-start(bf16[32,16,128]{2,1,0:T(8,128)(2,1)} %shard_map.127), channel_id=1, source_target_pairs={{0,16},{1,17},{2,18},{3,19},{4,20},{5,21},{6,22},{7,23},{8,24},{9,... | collective-permute-start | bytes 393224 | tf_op jit(solution)/shard_map/ppermute | solution.py:191

commit v2 on v1

v2 whole, which is shorter than its diff:
```python
import jax
import jax.numpy as jnp
from jax import lax
from jax.experimental import pallas as pl
from jax.experimental.pallas import tpu as pltpu
from jax.sharding import PartitionSpec as P

GROUP = 4
F32 = jnp.float32
BF16 = jnp.bfloat16


def vmem():
    return pl.BlockSpec(memory_space=pltpu.VMEM)


def smem():
    return pl.BlockSpec(memory_space=pltpu.SMEM)


def any_space():
    return pl.BlockSpec(memory_space=pl.ANY)


def OUT(shape, dtype):
    return pltpu.VMEM(shape, dtype)


def near(array):
    return pltpu.with_memory_space_constraint(array, pltpu.VMEM)


def low_lanes(shape):
    return lax.broadcasted_iota(jnp.int32, shape, len(shape) - 1) < shape[-1] // 2


def shard_scale(degree_ref, place):
    line = degree_ref[pl.ds(place // 2, 1), :]
    turned = pltpu.roll(line, 64, 1)
    first_half = place % 2 == 0
    low = low_lanes(line.shape)
    both = jnp.where(low == first_half, line, turned)
    return lax.rsqrt(both)


def pack_kernel(vectors_ref, degree_ref, out_ref):
    scale = shard_scale(degree_ref, lax.axis_index("row"))
    values = vectors_ref[...].astype(F32)
    half = values.shape[0] // 2
    wide = jnp.concatenate([values[:half], values[half:]], axis=1) * scale
    packed = wide.astype(BF16)
    for copy in range(out_ref.shape[0]):
        out_ref[copy] = packed


def unpack_source(source_ref, wide_ref):
    low = low_lanes((16, 128))
    for pair in range(source_ref.shape[0] // 2):
        even = source_ref[2 * pair].astype(F32)
        odd = source_ref[2 * pair + 1].astype(F32)
        top = jnp.where(low, even, pltpu.roll(odd, 64, 1))
        bottom = jnp.where(low, pltpu.roll(even, 64, 1), odd)
        lanes = slice(128 * (pair % 2), 128 * (pair % 2) + 128)
        wide_ref[pair // 2, 0:16, lanes] = top.astype(BF16)
        wide_ref[pair // 2, 16:32, lanes] = bottom.astype(BF16)


def pack_total(total_ref, out_ref):
    low = low_lanes((16, 128))
    for pair in range(out_ref.shape[0] // 2):
        lanes = slice(128 * (pair % 2), 128 * (pair % 2) + 128)
        top = total_ref[pair // 2, 0:16, lanes]
        bottom = total_ref[pair // 2, 16:32, lanes]
        even = jnp.where(low, top, pltpu.roll(bottom, 64, 1))
        odd = jnp.where(low, pltpu.roll(top, 64, 1), bottom)
        out_ref[2 * pair] = even.astype(out_ref.dtype)
        out_ref[2 * pair + 1] = odd.astype(out_ref.dtype)


def group_count(used):
    return (used + GROUP - 1) // GROUP


def tile_copy(tiles_ref, buffer_ref, sems, slot):
    return pltpu.make_async_copy(tiles_ref.at[slot], buffer_ref.at[slot], sems.at[slot])


def start_tiles(tiles_ref, buffer_ref, sems, used):
    def start(slot, carry):
        tile_copy(tiles_ref, buffer_ref, sems, slot).start()
        return carry

    lax.fori_loop(0, group_count(used) * GROUP, start, 0)


def add_tiles(in_at, out_at, used, wide_ref, total_ref, buffer_ref, flip, wait=None):
    contract = (((1,), (0,)), ((), ())) if flip else (((1,), (1,)), ((), ()))

    def body(group, carry):
        base = group * GROUP
        prods = []
        for step in range(GROUP):
            slot = base + step
            if wait is not None:
                wait(slot)
            prod = lax.dot_general(
                wide_ref[in_at(slot)], buffer_ref[slot], contract, preferred_element_type=F32
            )
            prods.append(jnp.where(slot < used, prod, 0.0))
        for step in range(GROUP):
            spot = out_at(base + step)
            total_ref[spot] = total_ref[spot] + prods[step]
        return carry

    lax.fori_loop(0, group_count(used), body, 0)


def own_kernel(
    rows_ref, cols_ref, count_ref, source_ref, tiles_ref, total_ref, wide_out_ref, buffer_ref, sems
):
    used = count_ref[0, 0]
    start_tiles(tiles_ref, buffer_ref, sems, used)
    total_ref[...] = jnp.zeros_like(total_ref)
    unpack_source(source_ref, wide_out_ref)
    add_tiles(
        lambda slot: cols_ref[0, 0, slot],
        lambda slot: rows_ref[0, 0, slot],
        used,
        wide_out_ref,
        total_ref,
        buffer_ref,
        False,
        lambda slot: tile_copy(tiles_ref, buffer_ref, sems, slot).wait(),
    )


def home_kernel(index_ref, wide_ref, home_ref, total_ref, out_ref, sum_ref):
    sum_ref[...] = total_ref[...]
    add_tiles(
        lambda slot: index_ref[1, slot],
        lambda slot: index_ref[0, slot],
        index_ref[2, 0],
        wide_ref,
        sum_ref,
        home_ref,
        False,
    )
    pack_total(sum_ref, out_ref)


def back_kernel(
    rows_ref,
    cols_ref,
    count_ref,
    index_ref,
    source_ref,
    tiles_ref,
    home_ref,
    out_ref,
    wide_ref,
    sum_ref,
    buffer_ref,
    sems,
):
    used = count_ref[0, 0]
    start_tiles(tiles_ref, buffer_ref, sems, used)
    sum_ref[...] = jnp.zeros_like(sum_ref)
    unpack_source(source_ref, wide_ref)
    add_tiles(
        lambda slot: rows_ref[0, 0, slot],
        lambda slot: cols_ref[0, 0, slot],
        used,
        wide_ref,
        sum_ref,
        buffer_ref,
        True,
        lambda slot: tile_copy(tiles_ref, buffer_ref, sems, slot).wait(),
    )
    add_tiles(
        lambda slot: index_ref[0, slot],
        lambda slot: index_ref[1, slot],
        index_ref[2, 0],
        wide_ref,
        sum_ref,
        home_ref,
        True,
    )
    pack_total(sum_ref, out_ref)


def sum_chunks(received_ref):
    parts = [received_ref[chunk].astype(F32) for chunk in range(received_ref.shape[0])]
    while len(parts) > 1:
        parts = [parts[k] + parts[k + 1] for k in range(0, len(parts), 2)]
    return parts[0]


def store_shard(out_ref, wide):
    out_ref[0:16, :] = wide[:, 0:64]
    out_ref[16:32, :] = pltpu.roll(wide, 64, 1)[:, 0:64]


def middle_kernel(received_ref, degree_ref, out_ref, copies_ref):
    wide = sum_chunks(received_ref) * shard_scale(degree_ref, lax.axis_index("col"))
    store_shard(out_ref, wide)
    packed = wide.astype(BF16)
    for copy in range(copies_ref.shape[0]):
        copies_ref[copy] = packed


def last_kernel(received_ref, degree_ref, out_ref):
    wide = sum_chunks(received_ref) * shard_scale(degree_ref, lax.axis_index("row"))
    store_shard(out_ref, wide)


def exchange(chunks, axis):
    return lax.all_to_all(chunks, axis, 0, 0, tiled=True)


def partner(block):
    count = lax.axis_size("col")
    return lax.ppermute(block, "col", [(k, k ^ (count // 2)) for k in range(count)])


def shards(
    vectors,
    row_degree,
    col_degree,
    tiles,
    tile_rows,
    tile_cols,
    tile_counts,
    lent_tiles,
    lent_rows,
    lent_cols,
    lent_counts,
):
    own = tiles.reshape(tiles.shape[2:])
    lent = lent_tiles.reshape(lent_tiles.shape[2:])
    slots, lents = own.shape[0], lent.shape[0]
    row_lines = row_degree.reshape(-1, 128)
    col_lines = col_degree.reshape(-1, 128)
    row_size, col_size = lax.axis_size("row"), lax.axis_size("col")
    chunk = (16, 128)
    wide = (row_degree.shape[0] // 256, 32, 256)

    index = jnp.stack(
        [
            lent_rows.reshape(-1),
            lent_cols.reshape(-1),
            jnp.broadcast_to(lent_counts.reshape(1), (lents,)),
        ]
    )
    home = near(partner(lent))
    home_index = partner(index)
    copies = pl.pallas_call(
        pack_kernel,
        out_shape=OUT((row_size,) + chunk, BF16),
        in_specs=[vmem(), vmem()],
        out_specs=vmem(),
    )(vectors.T, col_lines)
    source = exchange(copies, "row")
    total, wide_source = pl.pallas_call(
        own_kernel,
        out_shape=(OUT(wide, F32), OUT(wide, BF16)),
        in_specs=[smem(), smem(), smem(), vmem(), any_space()],
        out_specs=(vmem(), vmem()),
        scratch_shapes=[
            pltpu.VMEM(own.shape, BF16),
            pltpu.SemaphoreType.DMA((slots,)),
        ],
    )(tile_rows, tile_cols, tile_counts, near(source), own)
    partial_value = pl.pallas_call(
        home_kernel,
        out_shape=OUT((col_size,) + chunk, BF16),
        in_specs=[smem(), vmem(), vmem(), vmem()],
        out_specs=vmem(),
        scratch_shapes=[pltpu.VMEM(wide, F32)],
    )(home_index, near(wide_source), home, near(total))
    first, middle_copies = pl.pallas_call(
        middle_kernel,
        out_shape=(OUT((32, 64), F32), OUT((col_size,) + chunk, BF16)),
        in_specs=[vmem(), vmem()],
        out_specs=(vmem(), vmem()),
    )(near(exchange(partial_value, "col")), row_lines)
    middle = exchange(middle_copies, "col")
    partial_back = pl.pallas_call(
        back_kernel,
        out_shape=OUT((row_size,) + chunk, BF16),
        in_specs=[smem(), smem(), smem(), smem(), vmem(), any_space(), vmem()],
        out_specs=vmem(),
        scratch_shapes=[
            pltpu.VMEM(wide, BF16),
            pltpu.VMEM(wide, F32),
            pltpu.VMEM(own.shape, BF16),
            pltpu.SemaphoreType.DMA((slots,)),
        ],
    )(tile_rows, tile_cols, tile_counts, home_index, near(middle), own, home)
    second = pl.pallas_call(
        last_kernel,
        out_shape=jax.ShapeDtypeStruct((32, 64), F32),
        in_specs=[vmem(), vmem()],
        out_specs=vmem(),
    )(near(exchange(partial_back, "row")), col_lines)
    return (first.T, second.T)


def solution(mesh):
    return jax.shard_map(
        shards,
        mesh=mesh,
        in_specs=(
            P(("col", "row"), None),
            P("row"),
            P("col"),
            P("row", "col", None, None, None),
            P("row", "col", None),
            P("row", "col", None),
            P("row", "col"),
            P("row", "col", None, None, None),
            P("row", "col", None),
            P("row", "col", None),
            P("row", "col"),
        ),
        out_specs=(P(("row", "col"), None), P(("col", "row"), None)),
        check_vma=False,
    )
```

time: 128 us -> 112 us (0.88)
  the two profiles are of different devices: /device:TPU:8 before, /device:TPU:72 now
where the time goes in v2:
time: 112 us; the launch traced here: 111 us
  starting transfers between devices  37 us (33%)
  waiting for transfers between devices  33.9 us (30%)
  blocking collectives  26.3 us (23%)
  Pallas kernels  10.2 us (9%)
  between operations  2.01 us (2%)
  local copies, waits for them, and re-layouts  1.24 us (1%)
    all_to_all x2, waiting for transfers between devices, exchange(): return lax.all_to_all(chunks, axis, 0, 0, tiled=True)  33.9 us
    all_to_all x2, starting transfers between devices, exchange(): return lax.all_to_all(chunks, axis, 0, 0, tiled=True)  29.6 us
    all_to_all x2, blocking collectives, exchange(): return lax.all_to_all(chunks, axis, 0, 0, tiled=True)  26.3 us
    ppermute x2, starting transfers between devices, partner(): lax.ppermute(block, 'col', [(k, k ^ count // 2) for k in range(count)])  7.33 us
    pallas_call x1, Pallas kernels, shards(): pl.pallas_call(back_kernel, out_shape=OUT((row_size,) + chunk, BF16), in_...  3.14 us
    pallas_call x1, Pallas kernels, shards(): pl.pallas_call(own_kernel, out_shape=(OUT(wide, F32), OUT(wide, BF16)), i...  2.48 us
  transfers between devices with their start and end apart: 4, of which 2 were waited for; matrix products, arithmetic and copies ran while one was open for 1% of the time, Pallas kernels for 4%

profile of v2, /device:TPU:72, one launch (start us, length us, event | category | flops | bytes accessed | tf_op | source)
XLA Modules:
  0.0 111.4 jit_solution(8946478643980239839)
XLA Ops:
  0.6 4.9 %collective-permute-start.1 = (bf16[8,256,256]{2,1,0:T(8,128)(2,1)}, bf16[8,256,256]{2,1,0:T(8,128)(2,1)S(1)}, u32[]{:S(2)}, u32[]{:S(2)}) collective-permute-start(bf16[8,256,256]{2,1,0:T(8,128)(2,1)} %bitcast.23), channel_id=1, source_target_pairs={{0,16},{1,17},{2,18},{3,19},{4,20},{5,21},{6,22},{7,23},{8,24},{9,... | collective-permute-start | bytes 3145736 | tf_op jit(solution)/shard_map/ppermute | solution.py:222
  5.6 1.5 %shard_map.122 = bf16[32,16,128]{2,1,0:T(8,128)(2,1)} custom-call(bf16[32,64]{1,0:T(8,128)(2,1)} %bitcast.19, f32[16,128]{1,0:T(8,128)} %bitcast.16), custom_call_target="tpu_custom_call" | custom-call | tf_op jit(solution)/shard_map/pallas_call | solution.py:256
  7.0 23.7 %all-to-all-start = ((bf16[32,16,128]{2,1,0:T(8,128)(2,1)}), bf16[32,16,128]{2,1,0:T(8,128)(2,1)S(1)}, u32[]{:S(2)}, u32[]{:S(2)}) async-start(bf16[32,16,128]{2,1,0:T(8,128)(2,1)} %shard_map.122), calls=%async_computation | async-start | bytes 262144 | tf_op jit(solution)/shard_map/all_to_all | solution.py:217
  31.4 0.1 pad.2.clone
  31.4 0.7 add_add_fusion
  32.2 2.4 %collective-permute-start = (s32[3,8]{1,0:T(4,128)S(1)}, s32[3,8]{1,0:T(4,128)S(1)}, u32[]{:S(2)}, u32[]{:S(2)}) collective-permute-start(s32[3,8]{1,0:T(4,128)S(1)} %add_add_fusion), channel_id=1, source_target_pairs={{0,16},{1,17},{2,18},{3,19},{4,20},{5,21},{6,22},{7,23},{8,24},{9,... | collective-permute-start | bytes 296 | tf_op jit(solution)/shard_map/ppermute | solution.py:222
  35.2 14.4 %all-to-all-done.source_ref = bf16[32,16,128]{2,1,0:T(8,128)(2,1)S(1)} async-done(((bf16[32,16,128]{2,1,0:T(8,128)(2,1)}), bf16[32,16,128]{2,1,0:T(8,128)(2,1)S(1)}, u32[]{:S(2)}, u32[]{:S(2)}) %all-to-all-start) | async-done | bytes 131104 | tf_op jit(solution)/shard_map/all_to_all | solution.py:217
  49.7 2.5 %shard_map.123 = (f32[8,32,256]{2,1,0:T(8,128)S(1)}, bf16[8,32,256]{2,1,0:T(8,128)(2,1)S(1)}) custom-call(s32[1,1,16]{2,1,0:T(1,128)} %rows_ref.3, s32[1,1,16]{2,1,0:T(1,128)} %cols_ref.3, s32[1,1]{1,0:T(1,128)S(6)} %copy.14.count_ref, bf16[32,16,128]{2,1,0:T(8,128)(2,1)S(1)} %all-to-all-done.source_ref, bf16[16,256,256]{2,1,0:T(8,128)(2,1)} %bitcast.14), custom_call_target="tpu_custom_call" | custom-call | tf_op jit(solution)/shard_map/pallas_call | solution.py:263
  52.1 0.0 collective-permute-done.index_ref
  52.2 0.0 copy-start
  52.2 0.0 collective-permute-done.1.home_ref
  52.2 0.6 copy-done
  52.7 0.8 shard_map.124
  53.6 14.2 %all_to_all.20.received_ref = bf16[32,16,128]{2,1,0:T(8,128)(2,1)S(1)} all-to-all(bf16[32,16,128]{2,1,0:T(8,128)(2,1)S(1)} %shard_map.124), channel_id=1, replica_groups=mesh['row'=32,'col'=32] {'col'}, dimensions={0} | all-to-all | bytes 262144 | tf_op jit(solution)/shard_map/all_to_all | solution.py:217
  67.8 0.9 shard_map.125
  68.6 12.1 %all_to_all.21.source_ref = bf16[32,16,128]{2,1,0:T(8,128)(2,1)S(1)} all-to-all(bf16[32,16,128]{2,1,0:T(8,128)(2,1)S(1)} %get-tuple-element.9), channel_id=1, replica_groups=mesh['row'=32,'col'=32] {'col'}, dimensions={0} | all-to-all | bytes 262144 | tf_op jit(solution)/shard_map/all_to_all | solution.py:217
  80.7 3.1 %shard_map.126 = bf16[32,16,128]{2,1,0:T(8,128)(2,1)} custom-call(s32[1,1,16]{2,1,0:T(1,128)} %rows_ref.3, s32[1,1,16]{2,1,0:T(1,128)} %cols_ref.3, s32[1,1]{1,0:T(1,128)S(6)} %copy.14.count_ref, s32[3,8]{1,0:T(4,128)} %copy-done, bf16[32,16,128]{2,1,0:T(8,128)(2,1)S(1)} %all_to_all.21.source_ref, bf16[16,256,256]{2,1,0:T(8,128)(2,1)} %bitcast.15, ...), custom_call_target="tpu_custom_call" | custom-call | tf_op jit(solution)/shard_map/pallas_call | solution.py:287
  83.8 5.9 %all-to-all-start.3 = ((bf16[32,16,128]{2,1,0:T(8,128)(2,1)}), bf16[32,16,128]{2,1,0:T(8,128)(2,1)S(1)}, u32[]{:S(2)}, u32[]{:S(2)}) async-start(bf16[32,16,128]{2,1,0:T(8,128)(2,1)} %shard_map.126), calls=%async_computation.3 | async-start | bytes 262144 | tf_op jit(solution)/shard_map/all_to_all | solution.py:217
  89.8 0.6 copy.13
  90.4 19.5 %all-to-all-done.3.received_ref = bf16[32,16,128]{2,1,0:T(8,128)(2,1)S(1)} async-done(((bf16[32,16,128]{2,1,0:T(8,128)(2,1)}), bf16[32,16,128]{2,1,0:T(8,128)(2,1)S(1)}, u32[]{:S(2)}, u32[]{:S(2)}) %all-to-all-start.3) | async-done | bytes 131104 | tf_op jit(solution)/shard_map/all_to_all | solution.py:217
  109.9 1.5 %shard_map.127 = f32[32,64]{1,0:T(8,128)} custom-call(bf16[32,16,128]{2,1,0:T(8,128)(2,1)S(1)} %all-to-all-done.3.received_ref, f32[16,128]{1,0:T(8,128)} %bitcast.17), custom_call_target="tpu_custom_call" | custom-call | tf_op jit(solution)/shard_map/pallas_call | solution.py:299
Async XLA Ops:
  0.6 51.5 %collective-permute-start.1 = (bf16[8,256,256]{2,1,0:T(8,128)(2,1)}, bf16[8,256,256]{2,1,0:T(8,128)(2,1)S(1)}, u32[]{:S(2)}, u32[]{:S(2)}) collective-permute-start(bf16[8,256,256]{2,1,0:T(8,128)(2,1)} %bitcast.23), channel_id=1, source_target_pairs={{0,16},{1,17},{2,18},{3,19},{4,20},{5,21},{6,22},{7,23},{8,24},{9,... | collective-permute-start | bytes 3145736 | tf_op jit(solution)/shard_map/ppermute | solution.py:222
  7.0 42.6 %all-to-all-start = ((bf16[32,16,128]{2,1,0:T(8,128)(2,1)}), bf16[32,16,128]{2,1,0:T(8,128)(2,1)S(1)}, u32[]{:S(2)}, u32[]{:S(2)}) async-start(bf16[32,16,128]{2,1,0:T(8,128)(2,1)} %shard_map.122), calls=%async_computation | async-start | bytes 262144 | tf_op jit(solution)/shard_map/all_to_all | solution.py:217
  32.2 20.0 %collective-permute-start = (s32[3,8]{1,0:T(4,128)S(1)}, s32[3,8]{1,0:T(4,128)S(1)}, u32[]{:S(2)}, u32[]{:S(2)}) collective-permute-start(s32[3,8]{1,0:T(4,128)S(1)} %add_add_fusion), channel_id=1, source_target_pairs={{0,16},{1,17},{2,18},{3,19},{4,20},{5,21},{6,22},{7,23},{8,24},{9,... | collective-permute-start | bytes 296 | tf_op jit(solution)/shard_map/ppermute | solution.py:222
  52.2 0.6 copy-start
  83.8 26.1 %all-to-all-start.3 = ((bf16[32,16,128]{2,1,0:T(8,128)(2,1)}), bf16[32,16,128]{2,1,0:T(8,128)(2,1)S(1)}, u32[]{:S(2)}, u32[]{:S(2)}) async-start(bf16[32,16,128]{2,1,0:T(8,128)(2,1)} %shard_map.126), calls=%async_computation.3 | async-start | bytes 262144 | tf_op jit(solution)/shard_map/all_to_all | solution.py:217

commit v3 on v2

v3 whole, which is shorter than its diff:
```python
import jax
import jax.numpy as jnp
from jax import lax
from jax.experimental import pallas as pl
from jax.experimental.pallas import tpu as pltpu
from jax.sharding import PartitionSpec as P

GROUP = 8
SMALL = pltpu.CompilerParams(vmem_limit_bytes=4 * 1024 * 1024)
F32 = jnp.float32
BF16 = jnp.bfloat16


def vmem():
    return pl.BlockSpec(memory_space=pltpu.VMEM)


def smem():
    return pl.BlockSpec(memory_space=pltpu.SMEM)


def OUT(shape, dtype):
    return pltpu.VMEM(shape, dtype)


def near(array):
    return pltpu.with_memory_space_constraint(array, pltpu.VMEM)


def far(array):
    return pltpu.with_memory_space_constraint(array, pltpu.HBM)


def low_lanes(shape):
    return lax.broadcasted_iota(jnp.int32, shape, len(shape) - 1) < shape[-1] // 2


def shard_scale(degree_ref, place):
    line = degree_ref[pl.ds(place // 2, 1), :]
    turned = pltpu.roll(line, 64, 1)
    first_half = place % 2 == 0
    low = low_lanes(line.shape)
    both = jnp.where(low == first_half, line, turned)
    return lax.rsqrt(both)


def pack_kernel(vectors_ref, degree_ref, out_ref):
    scale = shard_scale(degree_ref, lax.axis_index("row"))
    values = vectors_ref[...].astype(F32)
    half = values.shape[0] // 2
    wide = jnp.concatenate([values[:half], values[half:]], axis=1) * scale
    packed = wide.astype(BF16)
    for copy in range(out_ref.shape[0]):
        out_ref[copy] = packed


def unpack_source(source_ref, wide_ref):
    low = low_lanes((16, 128))
    for pair in range(source_ref.shape[0] // 2):
        even = source_ref[2 * pair].astype(F32)
        odd = source_ref[2 * pair + 1].astype(F32)
        top = jnp.where(low, even, pltpu.roll(odd, 64, 1))
        bottom = jnp.where(low, pltpu.roll(even, 64, 1), odd)
        lanes = slice(128 * (pair % 2), 128 * (pair % 2) + 128)
        wide_ref[pair // 2, 0:16, lanes] = top.astype(BF16)
        wide_ref[pair // 2, 16:32, lanes] = bottom.astype(BF16)


def pack_total(total_ref, out_ref):
    low = low_lanes((16, 128))
    for pair in range(out_ref.shape[0] // 2):
        lanes = slice(128 * (pair % 2), 128 * (pair % 2) + 128)
        top = total_ref[pair // 2, 0:16, lanes]
        bottom = total_ref[pair // 2, 16:32, lanes]
        even = jnp.where(low, top, pltpu.roll(bottom, 64, 1))
        odd = jnp.where(low, pltpu.roll(top, 64, 1), bottom)
        out_ref[2 * pair] = even.astype(out_ref.dtype)
        out_ref[2 * pair + 1] = odd.astype(out_ref.dtype)


def add_tiles(in_at, out_at, used, wide_ref, total_ref, tiles_ref, flip):
    contract = (((1,), (0,)), ((), ())) if flip else (((1,), (1,)), ((), ()))

    def body(group, carry):
        base = group * GROUP
        prods = []
        for step in range(GROUP):
            slot = base + step
            prod = lax.dot_general(
                wide_ref[in_at(slot)], tiles_ref[slot], contract, preferred_element_type=F32
            )
            prods.append(jnp.where(slot < used, prod, 0.0))
        for step in range(GROUP):
            spot = out_at(base + step)
            total_ref[spot] = total_ref[spot] + prods[step]
        return carry

    lax.fori_loop(0, (used + GROUP - 1) // GROUP, body, 0)


def product_kernel(flip):
    def kernel(
        rows_ref, cols_ref, count_ref, index_ref, source_ref, tiles_ref, home_ref, out_ref, wide_ref, sum_ref
    ):
        sum_ref[...] = jnp.zeros_like(sum_ref)
        unpack_source(source_ref, wide_ref)
        own_row = lambda slot: rows_ref[0, 0, slot]
        own_col = lambda slot: cols_ref[0, 0, slot]
        home_row = lambda slot: index_ref[0, slot]
        home_col = lambda slot: index_ref[1, slot]
        if flip:
            own_in, own_out, home_in, home_out = own_row, own_col, home_row, home_col
        else:
            own_in, own_out, home_in, home_out = own_col, own_row, home_col, home_row
        add_tiles(own_in, own_out, count_ref[0, 0], wide_ref, sum_ref, tiles_ref, flip)
        add_tiles(home_in, home_out, index_ref[2, 0], wide_ref, sum_ref, home_ref, flip)
        pack_total(sum_ref, out_ref)

    return kernel


def product(rows, cols, count, index, source, tiles, home, flip):
    wide = (source.shape[0] // 4, 32, 256)
    return pl.pallas_call(
        product_kernel(flip),
        compiler_params=SMALL,
        out_shape=OUT(source.shape, BF16),
        in_specs=[smem(), smem(), smem(), smem(), vmem(), vmem(), vmem()],
        out_specs=vmem(),
        scratch_shapes=[pltpu.VMEM(wide, BF16), pltpu.VMEM(wide, F32)],
    )(rows, cols, count, index, near(source), near(tiles), home)


def load_kernel(tiles_ref, out_ref, sem):
    copy = pltpu.make_async_copy(tiles_ref, out_ref, sem)
    copy.start()
    copy.wait()


def load_tiles(tiles):
    return pl.pallas_call(
        load_kernel,
        compiler_params=SMALL,
        out_shape=OUT(tiles.shape, tiles.dtype),
        in_specs=[pl.BlockSpec(memory_space=pl.ANY)],
        out_specs=vmem(),
        scratch_shapes=[pltpu.SemaphoreType.DMA],
    )(tiles)


def sum_chunks(received_ref):
    parts = [received_ref[chunk].astype(F32) for chunk in range(received_ref.shape[0])]
    while len(parts) > 1:
        parts = [parts[k] + parts[k + 1] for k in range(0, len(parts), 2)]
    return parts[0]


def store_shard(out_ref, wide):
    out_ref[0:16, :] = wide[:, 0:64]
    out_ref[16:32, :] = pltpu.roll(wide, 64, 1)[:, 0:64]


def middle_kernel(received_ref, degree_ref, out_ref, copies_ref):
    wide = sum_chunks(received_ref) * shard_scale(degree_ref, lax.axis_index("col"))
    store_shard(out_ref, wide)
    packed = wide.astype(BF16)
    for copy in range(copies_ref.shape[0]):
        copies_ref[copy] = packed


def last_kernel(received_ref, degree_ref, out_ref):
    wide = sum_chunks(received_ref) * shard_scale(degree_ref, lax.axis_index("row"))
    store_shard(out_ref, wide)


def exchange(chunks, axis):
    return lax.all_to_all(chunks, axis, 0, 0, tiled=True)


def partner(block):
    count = lax.axis_size("col")
    return lax.ppermute(block, "col", [(k, k ^ (count // 2)) for k in range(count)])


def shards(
    vectors,
    row_degree,
    col_degree,
    tiles,
    tile_rows,
    tile_cols,
    tile_counts,
    lent_tiles,
    lent_rows,
    lent_cols,
    lent_counts,
):
    own = load_tiles(far(tiles.reshape(tiles.shape[2:])))
    lent = lent_tiles.reshape(lent_tiles.shape[2:])
    lents = lent.shape[0]
    tile_rows = far(tile_rows)
    tile_cols = far(tile_cols)
    row_lines = near(row_degree.reshape(-1, 128))
    col_lines = col_degree.reshape(-1, 128)
    row_size, col_size = lax.axis_size("row"), lax.axis_size("col")
    chunk = (16, 128)

    index = jnp.stack(
        [
            lent_rows.reshape(-1),
            lent_cols.reshape(-1),
            jnp.broadcast_to(lent_counts.reshape(1), (lents,)),
        ]
    )
    home = near(partner(lent))
    home_index = partner(index)
    copies = pl.pallas_call(
        pack_kernel,
        compiler_params=SMALL,
        out_shape=OUT((row_size,) + chunk, BF16),
        in_specs=[vmem(), vmem()],
        out_specs=vmem(),
    )(far(vectors.T), far(col_lines))
    source = exchange(copies, "row")
    partial_value = product(
        tile_rows, tile_cols, tile_counts, home_index, source, own, home, False
    )
    first, middle_copies = pl.pallas_call(
        middle_kernel,
        compiler_params=SMALL,
        out_shape=(OUT((32, 64), F32), OUT((col_size,) + chunk, BF16)),
        in_specs=[vmem(), vmem()],
        out_specs=(vmem(), vmem()),
    )(near(exchange(partial_value, "col")), row_lines)
    middle = exchange(middle_copies, "col")
    partial_back = product(
        tile_rows, tile_cols, tile_counts, home_index, middle, own, home, True
    )
    second = pl.pallas_call(
        last_kernel,
        compiler_params=SMALL,
        out_shape=jax.ShapeDtypeStruct((32, 64), F32),
        in_specs=[vmem(), vmem()],
        out_specs=vmem(),
    )(near(exchange(partial_back, "row")), near(col_lines))
    return (first.T, second.T)


def solution(mesh):
    return jax.shard_map(
        shards,
        mesh=mesh,
        in_specs=(
            P(("col", "row"), None),
            P("row"),
            P("col"),
            P("row", "col", None, None, None),
            P("row", "col", None),
            P("row", "col", None),
            P("row", "col"),
            P("row", "col", None, None, None),
            P("row", "col", None),
            P("row", "col", None),
            P("row", "col"),
        ),
        out_specs=(P(("row", "col"), None), P(("col", "row"), None)),
        check_vma=False,
    )
```

time: 112 us -> 106 us (0.946)
  Pallas kernels: 10.2 us -> 7.13 us
  blocking collectives: 26.3 us -> 24.6 us
  waiting for transfers between devices: 33.9 us -> 32.3 us
    all_to_all x2, waiting for transfers between devices: 33.9 us -> 30 us  [exchange(): return lax.all_to_all(chunks, axis, 0, 0, tiled=True)]
    pallas_call x6, Pallas kernels: 10.2 us -> 7.13 us  [the longest x2 3.15 us: product(): pl.pallas_call(product_kernel(flip), compiler_params=SMALL, out_shape=OUT...]
    ppermute x2, waiting for transfers between devices: 0.01 us -> 2.29 us  [partner(): lax.ppermute(block, 'col', [(k, k ^ count // 2) for k in range(count)])]
    all_to_all x2, blocking collectives: 26.3 us -> 24.6 us  [exchange(): return lax.all_to_all(chunks, axis, 0, 0, tiled=True)]
  transfers between devices with their start and end apart: 4 -> 4, of which waited for: 2 -> 3; matrix products, arithmetic and copies ran while one was open for 1% -> 1% of each run, Pallas kernels for 4% -> 3%
where the time goes in v3:
time: 106 us; the launch traced here: 105 us
  starting transfers between devices  38 us (36%)
  waiting for transfers between devices  32.3 us (30%)
  blocking collectives  24.6 us (23%)
  Pallas kernels  7.13 us (7%)
  between operations  1.99 us (2%)
    all_to_all x2, starting transfers between devices, exchange(): return lax.all_to_all(chunks, axis, 0, 0, tiled=True)  30.7 us
    all_to_all x2, waiting for transfers between devices, exchange(): return lax.all_to_all(chunks, axis, 0, 0, tiled=True)  30 us
    all_to_all x2, blocking collectives, exchange(): return lax.all_to_all(chunks, axis, 0, 0, tiled=True)  24.6 us
    ppermute x2, starting transfers between devices, partner(): lax.ppermute(block, 'col', [(k, k ^ count // 2) for k in range(count)])  7.33 us
    pallas_call x2, Pallas kernels, product(): pl.pallas_call(product_kernel(flip), compiler_params=SMALL, out_shape=OUT...  3.15 us
    ppermute x2, waiting for transfers between devices, partner(): lax.ppermute(block, 'col', [(k, k ^ count // 2) for k in range(count)])  2.29 us
  transfers between devices with their start and end apart: 4, of which 3 were waited for; matrix products, arithmetic and copies ran while one was open for 1% of the time, Pallas kernels for 3%

profile of v3, /device:TPU:72, one launch (start us, length us, event | category | flops | bytes accessed | tf_op | source)
XLA Modules:
  0.0 105.4 jit_solution(15126454733541105099)
XLA Ops:
  0.6 4.9 %collective-permute-start.1 = (bf16[8,256,256]{2,1,0:T(8,128)(2,1)}, bf16[8,256,256]{2,1,0:T(8,128)(2,1)S(1)}, u32[]{:S(2)}, u32[]{:S(2)}) collective-permute-start(bf16[8,256,256]{2,1,0:T(8,128)(2,1)} %bitcast.22), channel_id=1, source_target_pairs={{0,16},{1,17},{2,18},{3,19},{4,20},{5,21},{6,22},{7,23},{8,24},{9,... | collective-permute-start | bytes 3145736 | tf_op jit(solution)/shard_map/ppermute | solution.py:182
  5.6 1.5 %shard_map.122 = bf16[32,16,128]{2,1,0:T(8,128)(2,1)} custom-call(bf16[32,64]{1,0:T(8,128)(2,1)} %bitcast.19, f32[16,128]{1,0:T(8,128)} %bitcast.14), custom_call_target="tpu_custom_call" | custom-call | tf_op jit(solution)/shard_map/pallas_call | solution.py:217
  7.0 23.7 %all-to-all-start = ((bf16[32,16,128]{2,1,0:T(8,128)(2,1)}), bf16[32,16,128]{2,1,0:T(8,128)(2,1)S(1)}, u32[]{:S(2)}, u32[]{:S(2)}) async-start(bf16[32,16,128]{2,1,0:T(8,128)(2,1)} %shard_map.122), calls=%async_computation | async-start | bytes 262144 | tf_op jit(solution)/shard_map/all_to_all | solution.py:177
  31.4 0.1 pad.2.clone
  31.4 0.7 add_add_fusion
  32.2 2.4 %collective-permute-start = (s32[3,8]{1,0:T(4,128)S(1)}, s32[3,8]{1,0:T(4,128)S(1)}, u32[]{:S(2)}, u32[]{:S(2)}) collective-permute-start(s32[3,8]{1,0:T(4,128)S(1)} %add_add_fusion), channel_id=1, source_target_pairs={{0,16},{1,17},{2,18},{3,19},{4,20},{5,21},{6,22},{7,23},{8,24},{9,... | collective-permute-start | bytes 296 | tf_op jit(solution)/shard_map/ppermute | solution.py:182
  35.2 1.6 %shard_map.123.tiles_ref = bf16[16,256,256]{2,1,0:T(8,128)(2,1)S(1)} custom-call(bf16[16,256,256]{2,1,0:T(8,128)(2,1)} %bitcast.17), custom_call_target="tpu_custom_call" | custom-call | tf_op jit(solution)/shard_map/pallas_call | solution.py:141
  36.9 0.0 copy-start.1
  36.9 2.3 %collective-permute-done.index_ref = s32[3,8]{1,0:T(4,128)S(1)} collective-permute-done((s32[3,8]{1,0:T(4,128)S(1)}, s32[3,8]{1,0:T(4,128)S(1)}, u32[]{:S(2)}, u32[]{:S(2)}) %collective-permute-start) | collective-permute-done | bytes 128 | tf_op jit(solution)/shard_map/ppermute | solution.py:182
  39.2 10.5 %all-to-all-done.source_ref = bf16[32,16,128]{2,1,0:T(8,128)(2,1)S(1)} async-done(((bf16[32,16,128]{2,1,0:T(8,128)(2,1)}), bf16[32,16,128]{2,1,0:T(8,128)(2,1)S(1)}, u32[]{:S(2)}, u32[]{:S(2)}) %all-to-all-start) | async-done | bytes 131104 | tf_op jit(solution)/shard_map/all_to_all | solution.py:177
  49.7 0.0 collective-permute-done.1.home_ref
  49.7 1.3 %shard_map.124 = bf16[32,16,128]{2,1,0:T(8,128)(2,1)S(1)} custom-call(s32[1,1,16]{2,1,0:T(1,128)} %rows_ref.3, s32[1,1,16]{2,1,0:T(1,128)} %cols_ref.3, s32[1,1]{1,0:T(1,128)S(6)} %copy.14.count_ref, s32[3,8]{1,0:T(4,128)S(1)} %collective-permute-done.index_ref, bf16[32,16,128]{2,1,0:T(8,128)(2,1)S(1)} %all-to-all-done.source_ref, ...), custom_call_target="tpu_custom_call" | custom-call | tf_op jit(solution)/shard_map/pallas_call | solution.py:124
  51.0 12.5 %all_to_all.20.received_ref = bf16[32,16,128]{2,1,0:T(8,128)(2,1)S(1)} all-to-all(bf16[32,16,128]{2,1,0:T(8,128)(2,1)S(1)} %shard_map.124), channel_id=1, replica_groups=mesh['row'=32,'col'=32] {'col'}, dimensions={0} | all-to-all | bytes 262144 | tf_op jit(solution)/shard_map/all_to_all | solution.py:177
  63.5 0.0 copy-start
  63.5 0.0 copy-done.1
  63.5 0.2 shard_map.125
  63.7 12.1 %all_to_all.21.source_ref = bf16[32,16,128]{2,1,0:T(8,128)(2,1)S(1)} all-to-all(bf16[32,16,128]{2,1,0:T(8,128)(2,1)S(1)} %get-tuple-element.5), channel_id=1, replica_groups=mesh['row'=32,'col'=32] {'col'}, dimensions={0} | all-to-all | bytes 262144 | tf_op jit(solution)/shard_map/all_to_all | solution.py:177
  75.7 1.8 %shard_map.126 = bf16[32,16,128]{2,1,0:T(8,128)(2,1)} custom-call(s32[1,1,16]{2,1,0:T(1,128)} %rows_ref.3, s32[1,1,16]{2,1,0:T(1,128)} %cols_ref.3, s32[1,1]{1,0:T(1,128)S(6)} %copy.14.count_ref, s32[3,8]{1,0:T(4,128)S(1)} %collective-permute-done.index_ref, bf16[32,16,128]{2,1,0:T(8,128)(2,1)S(1)} %all_to_all.21.source_ref, ...), custom_call_target="tpu_custom_call" | custom-call | tf_op jit(solution)/shard_map/pallas_call | solution.py:124
  77.6 7.0 %all-to-all-start.3 = ((bf16[32,16,128]{2,1,0:T(8,128)(2,1)}), bf16[32,16,128]{2,1,0:T(8,128)(2,1)S(1)}, u32[]{:S(2)}, u32[]{:S(2)}) async-start(bf16[32,16,128]{2,1,0:T(8,128)(2,1)} %shard_map.126), calls=%async_computation.3 | async-start | bytes 262144 | tf_op jit(solution)/shard_map/all_to_all | solution.py:177
  84.5 0.6 copy.13
  85.2 19.5 %all-to-all-done.3.received_ref = bf16[32,16,128]{2,1,0:T(8,128)(2,1)S(1)} async-done(((bf16[32,16,128]{2,1,0:T(8,128)(2,1)}), bf16[32,16,128]{2,1,0:T(8,128)(2,1)S(1)}, u32[]{:S(2)}, u32[]{:S(2)}) %all-to-all-start.3) | async-done | bytes 131104 | tf_op jit(solution)/shard_map/all_to_all | solution.py:177
  104.7 0.0 copy-done
  104.7 0.8 shard_map.127
Async XLA Ops:
  0.6 49.0 %collective-permute-start.1 = (bf16[8,256,256]{2,1,0:T(8,128)(2,1)}, bf16[8,256,256]{2,1,0:T(8,128)(2,1)S(1)}, u32[]{:S(2)}, u32[]{:S(2)}) collective-permute-start(bf16[8,256,256]{2,1,0:T(8,128)(2,1)} %bitcast.22), channel_id=1, source_target_pairs={{0,16},{1,17},{2,18},{3,19},{4,20},{5,21},{6,22},{7,23},{8,24},{9,... | collective-permute-start | bytes 3145736 | tf_op jit(solution)/shard_map/ppermute | solution.py:182
  7.0 42.6 %all-to-all-start = ((bf16[32,16,128]{2,1,0:T(8,128)(2,1)}), bf16[32,16,128]{2,1,0:T(8,128)(2,1)S(1)}, u32[]{:S(2)}, u32[]{:S(2)}) async-start(bf16[32,16,128]{2,1,0:T(8,128)(2,1)} %shard_map.122), calls=%async_computation | async-start | bytes 262144 | tf_op jit(solution)/shard_map/all_to_all | solution.py:177
  32.2 7.0 %collective-permute-start = (s32[3,8]{1,0:T(4,128)S(1)}, s32[3,8]{1,0:T(4,128)S(1)}, u32[]{:S(2)}, u32[]{:S(2)}) collective-permute-start(s32[3,8]{1,0:T(4,128)S(1)} %add_add_fusion), channel_id=1, source_target_pairs={{0,16},{1,17},{2,18},{3,19},{4,20},{5,21},{6,22},{7,23},{8,24},{9,... | collective-permute-start | bytes 296 | tf_op jit(solution)/shard_map/ppermute | solution.py:182
  36.9 26.7 %copy-start.1 = (f32[2048]{0:T(1024)S(1)}, f32[2048]{0:T(1024)}, u32[]{:S(2)}) copy-start(f32[2048]{0:T(1024)} %param.12) | copy-start | bytes 24580
  63.5 41.2 %copy-start = (f32[2048]{0:T(1024)S(1)}, f32[2048]{0:T(1024)}, u32[]{:S(2)}) copy-start(f32[2048]{0:T(1024)} %param.13) | copy-start | bytes 24580
  77.6 27.1 %all-to-all-start.3 = ((bf16[32,16,128]{2,1,0:T(8,128)(2,1)}), bf16[32,16,128]{2,1,0:T(8,128)(2,1)S(1)}, u32[]{:S(2)}, u32[]{:S(2)}) async-start(bf16[32,16,128]{2,1,0:T(8,128)(2,1)} %shard_map.126), calls=%async_computation.3 | async-start | bytes 262144 | tf_op jit(solution)/shard_map/all_to_all | solution.py:177

commit v4 on v3

--- a/solution.py
+++ b/solution.py
@@ -98,10 +98,15 @@
     lax.fori_loop(0, (used + GROUP - 1) // GROUP, body, 0)
 
 
-def product_kernel(flip):
-    def kernel(
-        rows_ref, cols_ref, count_ref, index_ref, source_ref, tiles_ref, home_ref, out_ref, wide_ref, sum_ref
-    ):
+def product_kernel(flip, carried):
+    def kernel(*refs):
+        rows_ref, cols_ref, count_ref, index_ref, source_ref, tiles_ref, home_ref = refs[:7]
+        if carried:
+            kept_ref, out_ref, kept_out_ref, wide_ref, sum_ref, sem = refs[7:]
+            kept_copy = pltpu.make_async_copy(kept_ref, kept_out_ref, sem)
+            kept_copy.start()
+        else:
+            out_ref, wide_ref, sum_ref = refs[7:]
         sum_ref[...] = jnp.zeros_like(sum_ref)
         unpack_source(source_ref, wide_ref)
         own_row = lambda slot: rows_ref[0, 0, slot]
@@ -115,37 +120,59 @@
         add_tiles(own_in, own_out, count_ref[0, 0], wide_ref, sum_ref, tiles_ref, flip)
         add_tiles(home_in, home_out, index_ref[2, 0], wide_ref, sum_ref, home_ref, flip)
         pack_total(sum_ref, out_ref)
+        if carried:
+            kept_copy.wait()
 
     return kernel
 
 
-def product(rows, cols, count, index, source, tiles, home, flip):
+def product(rows, cols, count, index, source, tiles, home, flip, kept=None):
     wide = (source.shape[0] // 4, 32, 256)
+    operands = [rows, cols, count, index, near(source), near(tiles), home]
+    out_shape, out_specs = [OUT(source.shape, BF16)], [vmem()]
+    scratch = [pltpu.VMEM(wide, BF16), pltpu.VMEM(wide, F32)]
+    if kept is not None:
+        operands.append(near(kept))
+        out_shape.append(jax.ShapeDtypeStruct(kept.shape, kept.dtype))
+        out_specs.append(pl.BlockSpec(memory_space=pltpu.HBM))
+        scratch.append(pltpu.SemaphoreType.DMA)
     return pl.pallas_call(
-        product_kernel(flip),
-        compiler_params=SMALL,
-        out_shape=OUT(source.shape, BF16),
-        in_specs=[smem(), smem(), smem(), smem(), vmem(), vmem(), vmem()],
-        out_specs=vmem(),
-        scratch_shapes=[pltpu.VMEM(wide, BF16), pltpu.VMEM(wide, F32)],
-    )(rows, cols, count, index, near(source), near(tiles), home)
-
-
-def load_kernel(tiles_ref, out_ref, sem):
-    copy = pltpu.make_async_copy(tiles_ref, out_ref, sem)
-    copy.start()
-    copy.wait()
-
-
-def load_tiles(tiles):
+        product_kernel(flip, kept is not None),
+        compiler_params=SMALL,
+        out_shape=out_shape,
+        in_specs=[smem()] * 4 + [vmem()] * (len(operands) - 4),
+        out_specs=out_specs,
+        scratch_shapes=scratch,
+    )(*operands)
+
+
+def load_kernel(count_ref, tiles_ref, out_ref, sems):
+    used = count_ref[0, 0]
+
+    def copy(slot):
+        return pltpu.make_async_copy(tiles_ref.at[slot], out_ref.at[slot], sems.at[slot])
+
+    def start(slot, carry):
+        copy(slot).start()
+        return carry
+
+    def wait(slot, carry):
+        copy(slot).wait()
+        return carry
+
+    lax.fori_loop(0, used, start, 0)
+    lax.fori_loop(0, used, wait, 0)
+
+
+def load_tiles(count, tiles):
     return pl.pallas_call(
         load_kernel,
         compiler_params=SMALL,
         out_shape=OUT(tiles.shape, tiles.dtype),
-        in_specs=[pl.BlockSpec(memory_space=pl.ANY)],
+        in_specs=[smem(), pl.BlockSpec(memory_space=pltpu.HBM)],
         out_specs=vmem(),
-        scratch_shapes=[pltpu.SemaphoreType.DMA],
-    )(tiles)
+        scratch_shapes=[pltpu.SemaphoreType.DMA((tiles.shape[0],))],
+    )(count, tiles)
 
 
 def sum_chunks(received_ref):
@@ -195,7 +222,7 @@
     lent_cols,
     lent_counts,
 ):
-    own = load_tiles(far(tiles.reshape(tiles.shape[2:])))
+    own = load_tiles(tile_counts, far(tiles.reshape(tiles.shape[2:])))
     lent = lent_tiles.reshape(lent_tiles.shape[2:])
     lents = lent.shape[0]
     tile_rows = far(tile_rows)
@@ -222,10 +249,10 @@
         out_specs=vmem(),
     )(far(vectors.T), far(col_lines))
     source = exchange(copies, "row")
-    partial_value = product(
+    (partial_value,) = product(
         tile_rows, tile_cols, tile_counts, home_index, source, own, home, False
     )
-    first, middle_copies = pl.pallas_call(
+    first_near, middle_copies = pl.pallas_call(
         middle_kernel,
         compiler_params=SMALL,
         out_shape=(OUT((32, 64), F32), OUT((col_size,) + chunk, BF16)),
@@ -233,8 +260,8 @@
         out_specs=(vmem(), vmem()),
     )(near(exchange(partial_value, "col")), row_lines)
     middle = exchange(middle_copies, "col")
-    partial_back = product(
-        tile_rows, tile_cols, tile_counts, home_index, middle, own, home, True
+    partial_back, first = product(
+        tile_rows, tile_cols, tile_counts, home_index, middle, own, home, True, first_near
     )
     second = pl.pallas_call(
         last_kernel,

time: 106 us -> 106 us (level)
  blocking collectives: 24.6 us -> 51.1 us
  waiting for transfers between devices: 32.3 us -> 12.9 us
  starting transfers between devices: 38 us -> 31 us
    all_to_all x2 -> x3, blocking collectives: 24.6 us -> 51.1 us  [exchange(): return lax.all_to_all(chunks, axis, 0, 0, tiled=True)]
    all_to_all x2 -> x1, waiting for transfers between devices: 30 us -> 10.5 us  [exchange(): return lax.all_to_all(chunks, axis, 0, 0, tiled=True)]
    all_to_all x2 -> x1, starting transfers between devices: 30.7 us -> 23.7 us  [exchange(): return lax.all_to_all(chunks, axis, 0, 0, tiled=True)]
  transfers between devices with their start and end apart: 4 -> 3, of which waited for: 3 -> 2; matrix products, arithmetic and copies ran while one was open for 1% -> 1% of each run, Pallas kernels for 3% -> 3%
where the time goes in v4:
time: 106 us; the launch traced here: 105 us
  blocking collectives  51.1 us (48%)
  starting transfers between devices  31 us (29%)
  waiting for transfers between devices  12.9 us (12%)
  Pallas kernels  7.12 us (7%)
  between operations  1.99 us (2%)
    all_to_all x3, blocking collectives, exchange(): return lax.all_to_all(chunks, axis, 0, 0, tiled=True)  51.1 us
    all_to_all x1, starting transfers between devices, exchange(): return lax.all_to_all(chunks, axis, 0, 0, tiled=True)  23.7 us
    all_to_all x1, waiting for transfers between devices, exchange(): return lax.all_to_all(chunks, axis, 0, 0, tiled=True)  10.5 us
    ppermute x2, starting transfers between devices, partner(): lax.ppermute(block, 'col', [(k, k ^ count // 2) for k in range(count)])  7.33 us
    pallas_call x2, Pallas kernels, product(): pl.pallas_call(product_kernel(flip, kept is not None), compiler_params=SM...  3.23 us
    ppermute x2, waiting for transfers between devices, partner(): lax.ppermute(block, 'col', [(k, k ^ count // 2) for k in range(count)])  2.38 us
  transfers between devices with their start and end apart: 3, of which 2 were waited for; matrix products, arithmetic and copies ran while one was open for 1% of the time, Pallas kernels for 3%

profile of v4, /device:TPU:72, one launch (start us, length us, event | category | flops | bytes accessed | tf_op | source)
XLA Modules:
  0.0 105.0 jit_solution(17453687490013459876)
XLA Ops:
  0.6 4.9 %collective-permute-start.1 = (bf16[8,256,256]{2,1,0:T(8,128)(2,1)}, bf16[8,256,256]{2,1,0:T(8,128)(2,1)S(1)}, u32[]{:S(2)}, u32[]{:S(2)}) collective-permute-start(bf16[8,256,256]{2,1,0:T(8,128)(2,1)} %bitcast.21), channel_id=1, source_target_pairs={{0,16},{1,17},{2,18},{3,19},{4,20},{5,21},{6,22},{7,23},{8,24},{9,... | collective-permute-start | bytes 3145736 | tf_op jit(solution)/shard_map/ppermute | solution.py:209
  5.6 1.5 %shard_map.122 = bf16[32,16,128]{2,1,0:T(8,128)(2,1)} custom-call(bf16[32,64]{1,0:T(8,128)(2,1)} %bitcast.18, f32[16,128]{1,0:T(8,128)} %bitcast.13), custom_call_target="tpu_custom_call" | custom-call | tf_op jit(solution)/shard_map/pallas_call | solution.py:244
  7.0 23.7 %all-to-all-start = ((bf16[32,16,128]{2,1,0:T(8,128)(2,1)}), bf16[32,16,128]{2,1,0:T(8,128)(2,1)S(1)}, u32[]{:S(2)}, u32[]{:S(2)}) async-start(bf16[32,16,128]{2,1,0:T(8,128)(2,1)} %shard_map.122), calls=%async_computation | async-start | bytes 262144 | tf_op jit(solution)/shard_map/all_to_all | solution.py:204
  31.4 0.1 pad.2.clone
  31.4 0.7 add_add_fusion
  32.2 2.4 %collective-permute-start = (s32[3,8]{1,0:T(4,128)S(1)}, s32[3,8]{1,0:T(4,128)S(1)}, u32[]{:S(2)}, u32[]{:S(2)}) collective-permute-start(s32[3,8]{1,0:T(4,128)S(1)} %add_add_fusion), channel_id=1, source_target_pairs={{0,16},{1,17},{2,18},{3,19},{4,20},{5,21},{6,22},{7,23},{8,24},{9,... | collective-permute-start | bytes 296 | tf_op jit(solution)/shard_map/ppermute | solution.py:209
  35.2 1.5 %shard_map.123.refs_5_ = bf16[16,256,256]{2,1,0:T(8,128)(2,1)S(1)} custom-call(s32[1,1]{1,0:T(1,128)S(6)} %copy.13.count_ref.refs_2_, bf16[16,256,256]{2,1,0:T(8,128)(2,1)} %bitcast.16), custom_call_target="tpu_custom_call" | custom-call | tf_op jit(solution)/shard_map/pallas_call | solution.py:168
  36.8 0.0 copy-start.1
  36.8 2.4 %collective-permute-done.refs_3_ = s32[3,8]{1,0:T(4,128)S(1)} collective-permute-done((s32[3,8]{1,0:T(4,128)S(1)}, s32[3,8]{1,0:T(4,128)S(1)}, u32[]{:S(2)}, u32[]{:S(2)}) %collective-permute-start) | collective-permute-done | bytes 128 | tf_op jit(solution)/shard_map/ppermute | solution.py:209
  39.2 10.5 %all-to-all-done.refs_4_ = bf16[32,16,128]{2,1,0:T(8,128)(2,1)S(1)} async-done(((bf16[32,16,128]{2,1,0:T(8,128)(2,1)}), bf16[32,16,128]{2,1,0:T(8,128)(2,1)S(1)}, u32[]{:S(2)}, u32[]{:S(2)}) %all-to-all-start) | async-done | bytes 131104 | tf_op jit(solution)/shard_map/all_to_all | solution.py:204
  49.7 0.0 collective-permute-done.1.refs_6_
  49.7 1.7 %shard_map.124 = bf16[32,16,128]{2,1,0:T(8,128)(2,1)S(1)} custom-call(s32[1,1,16]{2,1,0:T(1,128)} %refs_0_.3, s32[1,1,16]{2,1,0:T(1,128)} %refs_1_.3, s32[1,1]{1,0:T(1,128)S(6)} %copy.13.count_ref.refs_2_, s32[3,8]{1,0:T(4,128)S(1)} %collective-permute-done.refs_3_, bf16[32,16,128]{2,1,0:T(8,128)(2,1)S(1)} %all-to-all-done.refs_4_, ...), custom_call_target="tpu_custom_call" | custom-call | tf_op jit(solution)/shard_map/pallas_call | solution.py:139
  51.4 0.0 copy-start
  51.4 12.1 %all_to_all.20.received_ref = bf16[32,16,128]{2,1,0:T(8,128)(2,1)S(1)} all-to-all(bf16[32,16,128]{2,1,0:T(8,128)(2,1)S(1)} %shard_map.124), channel_id=1, replica_groups=mesh['row'=32,'col'=32] {'col'}, dimensions={0} | all-to-all | bytes 262144 | tf_op jit(solution)/shard_map/all_to_all | solution.py:204
  63.5 0.0 copy-done.1
  63.5 0.2 shard_map.125
  63.7 12.1 %all_to_all.21.refs_4_ = bf16[32,16,128]{2,1,0:T(8,128)(2,1)S(1)} all-to-all(bf16[32,16,128]{2,1,0:T(8,128)(2,1)S(1)} %get-tuple-element.6), channel_id=1, replica_groups=mesh['row'=32,'col'=32] {'col'}, dimensions={0} | all-to-all | bytes 262144 | tf_op jit(solution)/shard_map/all_to_all | solution.py:204
  75.7 1.5 %shard_map.126 = (bf16[32,16,128]{2,1,0:T(8,128)(2,1)S(1)}, f32[32,64]{1,0:T(8,128)}) custom-call(s32[1,1,16]{2,1,0:T(1,128)} %refs_0_.3, s32[1,1,16]{2,1,0:T(1,128)} %refs_1_.3, s32[1,1]{1,0:T(1,128)S(6)} %copy.13.count_ref.refs_2_, s32[3,8]{1,0:T(4,128)S(1)} %collective-permute-done.refs_3_, bf16[32,16,128]{2,1,0:T(8,128)(2,1)S(1)} %all_to_all.21.refs_4_, ...), custom_call_target="tpu_custom_call" | custom-call | tf_op jit(solution)/shard_map/pallas_call | solution.py:139
  77.2 27.0 %all_to_all.22.received_ref = bf16[32,16,128]{2,1,0:T(8,128)(2,1)S(1)} all-to-all(bf16[32,16,128]{2,1,0:T(8,128)(2,1)S(1)} %get-tuple-element.9), channel_id=1, replica_groups=mesh['row'=32,'col'=32] {'row'}, dimensions={0} | all-to-all | bytes 262144 | tf_op jit(solution)/shard_map/all_to_all | solution.py:204
  104.2 0.0 copy-done
  104.2 0.8 shard_map.127
Async XLA Ops:
  0.6 49.0 %collective-permute-start.1 = (bf16[8,256,256]{2,1,0:T(8,128)(2,1)}, bf16[8,256,256]{2,1,0:T(8,128)(2,1)S(1)}, u32[]{:S(2)}, u32[]{:S(2)}) collective-permute-start(bf16[8,256,256]{2,1,0:T(8,128)(2,1)} %bitcast.21), channel_id=1, source_target_pairs={{0,16},{1,17},{2,18},{3,19},{4,20},{5,21},{6,22},{7,23},{8,24},{9,... | collective-permute-start | bytes 3145736 | tf_op jit(solution)/shard_map/ppermute | solution.py:209
  7.0 42.6 %all-to-all-start = ((bf16[32,16,128]{2,1,0:T(8,128)(2,1)}), bf16[32,16,128]{2,1,0:T(8,128)(2,1)S(1)}, u32[]{:S(2)}, u32[]{:S(2)}) async-start(bf16[32,16,128]{2,1,0:T(8,128)(2,1)} %shard_map.122), calls=%async_computation | async-start | bytes 262144 | tf_op jit(solution)/shard_map/all_to_all | solution.py:204
  32.2 7.0 %collective-permute-start = (s32[3,8]{1,0:T(4,128)S(1)}, s32[3,8]{1,0:T(4,128)S(1)}, u32[]{:S(2)}, u32[]{:S(2)}) collective-permute-start(s32[3,8]{1,0:T(4,128)S(1)} %add_add_fusion), channel_id=1, source_target_pairs={{0,16},{1,17},{2,18},{3,19},{4,20},{5,21},{6,22},{7,23},{8,24},{9,... | collective-permute-start | bytes 296 | tf_op jit(solution)/shard_map/ppermute | solution.py:209
  36.8 26.7 %copy-start.1 = (f32[2048]{0:T(1024)S(1)}, f32[2048]{0:T(1024)}, u32[]{:S(2)}) copy-start(f32[2048]{0:T(1024)} %param.12) | copy-start | bytes 24580
  51.4 52.8 %copy-start = (f32[2048]{0:T(1024)S(1)}, f32[2048]{0:T(1024)}, u32[]{:S(2)}) copy-start(f32[2048]{0:T(1024)} %param.13) | copy-start | bytes 24580

commit v5 on v4

--- a/solution.py
+++ b/solution.py
@@ -44,7 +44,12 @@
     return lax.rsqrt(both)
 
 
-def pack_kernel(vectors_ref, degree_ref, out_ref):
+def pack_kernel(
+    vectors_ref, degree_ref, lent_rows_ref, lent_cols_ref, lent_count_ref, out_ref, index_ref
+):
+    index_ref[0:1, :] = lent_rows_ref[0]
+    index_ref[1:2, :] = lent_cols_ref[0]
+    index_ref[2:3, :] = jnp.full((1, index_ref.shape[1]), lent_count_ref[0, 0], jnp.int32)
     scale = shard_scale(degree_ref, lax.axis_index("row"))
     values = vectors_ref[...].astype(F32)
     half = values.shape[0] // 2
@@ -232,22 +237,15 @@
     row_size, col_size = lax.axis_size("row"), lax.axis_size("col")
     chunk = (16, 128)
 
-    index = jnp.stack(
-        [
-            lent_rows.reshape(-1),
-            lent_cols.reshape(-1),
-            jnp.broadcast_to(lent_counts.reshape(1), (lents,)),
-        ]
-    )
     home = near(partner(lent))
+    copies, index = pl.pallas_call(
+        pack_kernel,
+        compiler_params=SMALL,
+        out_shape=(OUT((row_size,) + chunk, BF16), OUT((3, lents), jnp.int32)),
+        in_specs=[vmem()] * 4 + [smem()],
+        out_specs=(vmem(), vmem()),
+    )(far(vectors.T), far(col_lines), far(lent_rows), far(lent_cols), lent_counts)
     home_index = partner(index)
-    copies = pl.pallas_call(
-        pack_kernel,
-        compiler_params=SMALL,
-        out_shape=OUT((row_size,) + chunk, BF16),
-        in_specs=[vmem(), vmem()],
-        out_specs=vmem(),
-    )(far(vectors.T), far(col_lines))
     source = exchange(copies, "row")
     (partial_value,) = product(
         tile_rows, tile_cols, tile_counts, home_index, source, own, home, False

time: 106 us -> 104 us (0.981)
  waiting for transfers between devices: 12.9 us -> 14.4 us
  blocking collectives: 51.1 us -> 50 us
    all_to_all x1, waiting for transfers between devices: 10.5 us -> 11.9 us  [exchange(): return lax.all_to_all(chunks, axis, 0, 0, tiled=True)]
    all_to_all x3, blocking collectives: 51.1 us -> 50 us  [exchange(): return lax.all_to_all(chunks, axis, 0, 0, tiled=True)]
  transfers between devices with their start and end apart: 3 -> 3, of which waited for: 2 -> 2; matrix products, arithmetic and copies ran while one was open for 1% -> 0% of each run, Pallas kernels for 3% -> 3%
where the time goes in v5:
time: 104 us
  blocking collectives  50 us (48%)
  starting transfers between devices  31 us (30%)
  waiting for transfers between devices  14.4 us (14%)
  Pallas kernels  6.38 us (6%)
  between operations  1.99 us (2%)
    all_to_all x3, blocking collectives, exchange(): return lax.all_to_all(chunks, axis, 0, 0, tiled=True)  50 us
    all_to_all x1, starting transfers between devices, exchange(): return lax.all_to_all(chunks, axis, 0, 0, tiled=True)  23.7 us
    all_to_all x1, waiting for transfers between devices, exchange(): return lax.all_to_all(chunks, axis, 0, 0, tiled=True)  11.9 us
    ppermute x2, starting transfers between devices, partner(): lax.ppermute(block, 'col', [(k, k ^ count // 2) for k in range(count)])  7.35 us
    pallas_call x2, Pallas kernels, product(): pl.pallas_call(product_kernel(flip, kept is not None), compiler_params=SM...  2.61 us
    ppermute x2, waiting for transfers between devices, partner(): lax.ppermute(block, 'col', [(k, k ^ count // 2) for k in range(count)])  2.5 us
  transfers between devices with their start and end apart: 3, of which 2 were waited for; matrix products, arithmetic and copies ran while one was open for 0% of the time, Pallas kernels for 3%

profile of v5, /device:TPU:72, one launch (start us, length us, event | category | flops | bytes accessed | tf_op | source)
XLA Modules:
  0.0 103.8 jit_solution(9781078378258056443)
XLA Ops:
  0.6 4.9 %collective-permute-start.1 = (bf16[8,256,256]{2,1,0:T(8,128)(2,1)}, bf16[8,256,256]{2,1,0:T(8,128)(2,1)S(1)}, u32[]{:S(2)}, u32[]{:S(2)}) collective-permute-start(bf16[8,256,256]{2,1,0:T(8,128)(2,1)} %bitcast.13), channel_id=1, source_target_pairs={{0,16},{1,17},{2,18},{3,19},{4,20},{5,21},{6,22},{7,23},{8,24},{9,... | collective-permute-start | bytes 3145736 | tf_op jit(solution)/shard_map/ppermute | solution.py:214
  6.2 1.5 %shard_map.122 = (bf16[32,16,128]{2,1,0:T(8,128)(2,1)}, s32[3,8]{1,0:T(4,128)S(1)}) custom-call(bf16[32,64]{1,0:T(8,128)(2,1)} %bitcast.12, f32[16,128]{1,0:T(8,128)} %bitcast.7, s32[1,1,8]{2,1,0:T(1,128)} %lent_rows_ref.1, s32[1,1,8]{2,1,0:T(1,128)} %lent_cols_ref.1, s32[1,1]{1,0:T(1,128)S(6)} %copy.14.lent_count_ref), custom_call_target="tpu_custom_call" | custom-call | tf_op jit(solution)/shard_map/pallas_call | solution.py:241
  7.7 23.7 %all-to-all-start = ((bf16[32,16,128]{2,1,0:T(8,128)(2,1)}), bf16[32,16,128]{2,1,0:T(8,128)(2,1)S(1)}, u32[]{:S(2)}, u32[]{:S(2)}) async-start(bf16[32,16,128]{2,1,0:T(8,128)(2,1)} %get-tuple-element.9), calls=%async_computation | async-start | bytes 262144 | tf_op jit(solution)/shard_map/all_to_all | solution.py:209
  31.4 2.4 %collective-permute-start = (s32[3,8]{1,0:T(4,128)S(1)}, s32[3,8]{1,0:T(4,128)S(1)}, u32[]{:S(2)}, u32[]{:S(2)}) collective-permute-start(s32[3,8]{1,0:T(4,128)S(1)} %get-tuple-element.8), channel_id=1, source_target_pairs={{0,16},{1,17},{2,18},{3,19},{4,20},{5,21},{6,22},{7,23},{8,24},{9,... | collective-permute-start | bytes 296 | tf_op jit(solution)/shard_map/ppermute | solution.py:214
  34.4 1.4 %shard_map.123.refs_5_ = bf16[16,256,256]{2,1,0:T(8,128)(2,1)S(1)} custom-call(s32[1,1]{1,0:T(1,128)S(6)} %copy.13.count_ref.refs_2_, bf16[16,256,256]{2,1,0:T(8,128)(2,1)} %bitcast.10), custom_call_target="tpu_custom_call" | custom-call | tf_op jit(solution)/shard_map/pallas_call | solution.py:173
  35.8 0.0 copy-start.1
  35.9 2.5 %collective-permute-done.refs_3_ = s32[3,8]{1,0:T(4,128)S(1)} collective-permute-done((s32[3,8]{1,0:T(4,128)S(1)}, s32[3,8]{1,0:T(4,128)S(1)}, u32[]{:S(2)}, u32[]{:S(2)}) %collective-permute-start) | collective-permute-done | bytes 128 | tf_op jit(solution)/shard_map/ppermute | solution.py:214
  38.4 11.9 %all-to-all-done.refs_4_ = bf16[32,16,128]{2,1,0:T(8,128)(2,1)S(1)} async-done(((bf16[32,16,128]{2,1,0:T(8,128)(2,1)}), bf16[32,16,128]{2,1,0:T(8,128)(2,1)S(1)}, u32[]{:S(2)}, u32[]{:S(2)}) %all-to-all-start) | async-done | bytes 131104 | tf_op jit(solution)/shard_map/all_to_all | solution.py:209
  50.3 0.0 collective-permute-done.1.refs_6_
  50.3 1.3 %shard_map.124 = bf16[32,16,128]{2,1,0:T(8,128)(2,1)S(1)} custom-call(s32[1,1,16]{2,1,0:T(1,128)} %refs_0_.3, s32[1,1,16]{2,1,0:T(1,128)} %refs_1_.3, s32[1,1]{1,0:T(1,128)S(6)} %copy.13.count_ref.refs_2_, s32[3,8]{1,0:T(4,128)S(1)} %collective-permute-done.refs_3_, bf16[32,16,128]{2,1,0:T(8,128)(2,1)S(1)} %all-to-all-done.refs_4_, ...), custom_call_target="tpu_custom_call" | custom-call | tf_op jit(solution)/shard_map/pallas_call | solution.py:144
  51.6 0.0 copy-start
  51.6 12.5 %all_to_all.20.received_ref = bf16[32,16,128]{2,1,0:T(8,128)(2,1)S(1)} all-to-all(bf16[32,16,128]{2,1,0:T(8,128)(2,1)S(1)} %shard_map.124), channel_id=1, replica_groups=mesh['row'=32,'col'=32] {'col'}, dimensions={0} | all-to-all | bytes 262144 | tf_op jit(solution)/shard_map/all_to_all | solution.py:209
  64.2 0.0 copy-done.1
  64.2 0.2 shard_map.125
  64.3 12.1 %all_to_all.21.refs_4_ = bf16[32,16,128]{2,1,0:T(8,128)(2,1)S(1)} all-to-all(bf16[32,16,128]{2,1,0:T(8,128)(2,1)S(1)} %get-tuple-element.10), channel_id=1, replica_groups=mesh['row'=32,'col'=32] {'col'}, dimensions={0} | all-to-all | bytes 262144 | tf_op jit(solution)/shard_map/all_to_all | solution.py:209
  76.4 1.3 %shard_map.126 = (bf16[32,16,128]{2,1,0:T(8,128)(2,1)S(1)}, f32[32,64]{1,0:T(8,128)}) custom-call(s32[1,1,16]{2,1,0:T(1,128)} %refs_0_.3, s32[1,1,16]{2,1,0:T(1,128)} %refs_1_.3, s32[1,1]{1,0:T(1,128)S(6)} %copy.13.count_ref.refs_2_, s32[3,8]{1,0:T(4,128)S(1)} %collective-permute-done.refs_3_, bf16[32,16,128]{2,1,0:T(8,128)(2,1)S(1)} %all_to_all.21.refs_4_, ...), custom_call_target="tpu_custom_call" | custom-call | tf_op jit(solution)/shard_map/pallas_call | solution.py:144
  77.7 25.4 %all_to_all.22.received_ref = bf16[32,16,128]{2,1,0:T(8,128)(2,1)S(1)} all-to-all(bf16[32,16,128]{2,1,0:T(8,128)(2,1)S(1)} %get-tuple-element.13), channel_id=1, replica_groups=mesh['row'=32,'col'=32] {'row'}, dimensions={0} | all-to-all | bytes 262144 | tf_op jit(solution)/shard_map/all_to_all | solution.py:209
  103.1 0.0 copy-done
  103.1 0.8 shard_map.127
Async XLA Ops:
  0.6 49.7 %collective-permute-start.1 = (bf16[8,256,256]{2,1,0:T(8,128)(2,1)}, bf16[8,256,256]{2,1,0:T(8,128)(2,1)S(1)}, u32[]{:S(2)}, u32[]{:S(2)}) collective-permute-start(bf16[8,256,256]{2,1,0:T(8,128)(2,1)} %bitcast.13), channel_id=1, source_target_pairs={{0,16},{1,17},{2,18},{3,19},{4,20},{5,21},{6,22},{7,23},{8,24},{9,... | collective-permute-start | bytes 3145736 | tf_op jit(solution)/shard_map/ppermute | solution.py:214
  7.7 42.6 %all-to-all-start = ((bf16[32,16,128]{2,1,0:T(8,128)(2,1)}), bf16[32,16,128]{2,1,0:T(8,128)(2,1)S(1)}, u32[]{:S(2)}, u32[]{:S(2)}) async-start(bf16[32,16,128]{2,1,0:T(8,128)(2,1)} %get-tuple-element.9), calls=%async_computation | async-start | bytes 262144 | tf_op jit(solution)/shard_map/all_to_all | solution.py:209
  31.4 7.0 %collective-permute-start = (s32[3,8]{1,0:T(4,128)S(1)}, s32[3,8]{1,0:T(4,128)S(1)}, u32[]{:S(2)}, u32[]{:S(2)}) collective-permute-start(s32[3,8]{1,0:T(4,128)S(1)} %get-tuple-element.8), channel_id=1, source_target_pairs={{0,16},{1,17},{2,18},{3,19},{4,20},{5,21},{6,22},{7,23},{8,24},{9,... | collective-permute-start | bytes 296 | tf_op jit(solution)/shard_map/ppermute | solution.py:214
  35.8 28.3 %copy-start.1 = (f32[2048]{0:T(1024)S(1)}, f32[2048]{0:T(1024)}, u32[]{:S(2)}) copy-start(f32[2048]{0:T(1024)} %param.12) | copy-start | bytes 24580
  51.6 51.4 %copy-start = (f32[2048]{0:T(1024)S(1)}, f32[2048]{0:T(1024)}, u32[]{:S(2)}) copy-start(f32[2048]{0:T(1024)} %param.13) | copy-start | bytes 24580

commit v6 on v4

--- a/solution.py
+++ b/solution.py
@@ -98,52 +98,111 @@
     lax.fori_loop(0, (used + GROUP - 1) // GROUP, body, 0)
 
 
-def product_kernel(flip, carried):
-    def kernel(*refs):
-        rows_ref, cols_ref, count_ref, index_ref, source_ref, tiles_ref, home_ref = refs[:7]
-        if carried:
-            kept_ref, out_ref, kept_out_ref, wide_ref, sum_ref, sem = refs[7:]
-            kept_copy = pltpu.make_async_copy(kept_ref, kept_out_ref, sem)
-            kept_copy.start()
-        else:
-            out_ref, wide_ref, sum_ref = refs[7:]
-        sum_ref[...] = jnp.zeros_like(sum_ref)
-        unpack_source(source_ref, wide_ref)
-        own_row = lambda slot: rows_ref[0, 0, slot]
-        own_col = lambda slot: cols_ref[0, 0, slot]
-        home_row = lambda slot: index_ref[0, slot]
-        home_col = lambda slot: index_ref[1, slot]
-        if flip:
-            own_in, own_out, home_in, home_out = own_row, own_col, home_row, home_col
-        else:
-            own_in, own_out, home_in, home_out = own_col, own_row, home_col, home_row
-        add_tiles(own_in, own_out, count_ref[0, 0], wide_ref, sum_ref, tiles_ref, flip)
-        add_tiles(home_in, home_out, index_ref[2, 0], wide_ref, sum_ref, home_ref, flip)
-        pack_total(sum_ref, out_ref)
-        if carried:
-            kept_copy.wait()
-
-    return kernel
-
-
-def product(rows, cols, count, index, source, tiles, home, flip, kept=None):
+def own_kernel(rows_ref, cols_ref, count_ref, source_ref, tiles_ref, sum_ref, wide_ref):
+    sum_ref[...] = jnp.zeros_like(sum_ref)
+    unpack_source(source_ref, wide_ref)
+    add_tiles(
+        lambda slot: cols_ref[0, 0, slot],
+        lambda slot: rows_ref[0, 0, slot],
+        count_ref[0, 0],
+        wide_ref,
+        sum_ref,
+        tiles_ref,
+        False,
+    )
+
+
+def home_kernel(index_ref, wide_ref, home_ref, own_sum_ref, out_ref, sum_ref):
+    sum_ref[...] = own_sum_ref[...]
+    add_tiles(
+        lambda slot: index_ref[1, slot],
+        lambda slot: index_ref[0, slot],
+        index_ref[2, 0],
+        wide_ref,
+        sum_ref,
+        home_ref,
+        False,
+    )
+    pack_total(sum_ref, out_ref)
+
+
+def forth(rows, cols, count, index, source, tiles, home):
     wide = (source.shape[0] // 4, 32, 256)
-    operands = [rows, cols, count, index, near(source), near(tiles), home]
-    out_shape, out_specs = [OUT(source.shape, BF16)], [vmem()]
-    scratch = [pltpu.VMEM(wide, BF16), pltpu.VMEM(wide, F32)]
-    if kept is not None:
-        operands.append(near(kept))
-        out_shape.append(jax.ShapeDtypeStruct(kept.shape, kept.dtype))
-        out_specs.append(pl.BlockSpec(memory_space=pltpu.HBM))
-        scratch.append(pltpu.SemaphoreType.DMA)
+    own_sum, wide_source = pl.pallas_call(
+        own_kernel,
+        compiler_params=SMALL,
+        out_shape=(OUT(wide, F32), OUT(wide, BF16)),
+        in_specs=[smem()] * 3 + [vmem()] * 2,
+        out_specs=(vmem(), vmem()),
+    )(rows, cols, count, near(source), near(tiles))
     return pl.pallas_call(
-        product_kernel(flip, kept is not None),
-        compiler_params=SMALL,
-        out_shape=out_shape,
-        in_specs=[smem()] * 4 + [vmem()] * (len(operands) - 4),
-        out_specs=out_specs,
-        scratch_shapes=scratch,
-    )(*operands)
+        home_kernel,
+        compiler_params=SMALL,
+        out_shape=OUT(source.shape, BF16),
+        in_specs=[smem()] + [vmem()] * 3,
+        out_specs=vmem(),
+        scratch_shapes=[pltpu.VMEM(wide, F32)],
+    )(index, near(wide_source), home, near(own_sum))
+
+
+def back_kernel(
+    rows_ref,
+    cols_ref,
+    count_ref,
+    index_ref,
+    source_ref,
+    tiles_ref,
+    home_ref,
+    kept_ref,
+    out_ref,
+    kept_out_ref,
+    wide_ref,
+    sum_ref,
+    sem,
+):
+    kept_copy = pltpu.make_async_copy(kept_ref, kept_out_ref, sem)
+    kept_copy.start()
+    sum_ref[...] = jnp.zeros_like(sum_ref)
+    unpack_source(source_ref, wide_ref)
+    add_tiles(
+        lambda slot: rows_ref[0, 0, slot],
+        lambda slot: cols_ref[0, 0, slot],
+        count_ref[0, 0],
+        wide_ref,
+        sum_ref,
+        tiles_ref,
+        True,
+    )
+    add_tiles(
+        lambda slot: index_ref[0, slot],
+        lambda slot: index_ref[1, slot],
+        index_ref[2, 0],
+        wide_ref,
+        sum_ref,
+        home_ref,
+        True,
+    )
+    pack_total(sum_ref, out_ref)
+    kept_copy.wait()
+
+
+def back(rows, cols, count, index, source, tiles, home, kept):
+    wide = (source.shape[0] // 4, 32, 256)
+    return pl.pallas_call(
+        back_kernel,
+        compiler_params=SMALL,
+        out_shape=(
+            OUT(source.shape, BF16),
+            jax.ShapeDtypeStruct(kept.shape, kept.dtype),
+        ),
+        in_specs=[smem()] * 4 + [vmem()] * 4,
+        out_specs=(vmem(), pl.BlockSpec(memory_space=pltpu.HBM)),
+        scratch_shapes=[
+            pltpu.VMEM(wide, BF16),
+            pltpu.VMEM(wide, F32),
+            pltpu.SemaphoreType.DMA,
+        ],
+    )(rows, cols, count, index, near(source), near(tiles), home, near(kept))
 
 
 def load_kernel(count_ref, tiles_ref, out_ref, sems):
@@ -249,9 +308,7 @@
         out_specs=vmem(),
     )(far(vectors.T), far(col_lines))
     source = exchange(copies, "row")
-    (partial_value,) = product(
-        tile_rows, tile_cols, tile_counts, home_index, source, own, home, False
-    )
+    partial_value = forth(tile_rows, tile_cols, tile_counts, home_index, source, own, home)
     first_near, middle_copies = pl.pallas_call(
         middle_kernel,
         compiler_params=SMALL,
@@ -260,8 +317,8 @@
         out_specs=(vmem(), vmem()),
     )(near(exchange(partial_value, "col")), row_lines)
     middle = exchange(middle_copies, "col")
-    partial_back, first = product(
-        tile_rows, tile_cols, tile_counts, home_index, middle, own, home, True, first_near
+    partial_back, first = back(
+        tile_rows, tile_cols, tile_counts, home_index, middle, own, home, first_near
     )
     second = pl.pallas_call(
         last_kernel,

time: 106 us -> 105 us (level)
  blocking collectives: 51.1 us -> 49.9 us
    all_to_all x1, waiting for transfers between devices: 10.5 us -> 12.9 us  [exchange(): return lax.all_to_all(chunks, axis, 0, 0, tiled=True)]
    ppermute x2, waiting for transfers between devices: 2.38 us -> 0.01 us  [partner(): lax.ppermute(block, 'col', [(k, k ^ count // 2) for k in range(count)])]
    all_to_all x3, blocking collectives: 51.1 us -> 49.9 us  [exchange(): return lax.all_to_all(chunks, axis, 0, 0, tiled=True)]
    pallas_call x2 -> x3, Pallas kernels: 3.23 us -> 3.8 us  [the longest x1 1.62 us: forth(): pl.pallas_call(own_kernel, compiler_params=SMALL, out_shape=(OUT(wide, F3...]
  transfers between devices with their start and end apart: 3 -> 3, of which waited for: 2 -> 1; matrix products, arithmetic and copies ran while one was open for 1% -> 1% of each run, Pallas kernels for 3% -> 4%
where the time goes in v6:
time: 105 us; the launch traced here: 104 us
  blocking collectives  49.9 us (48%)
  starting transfers between devices  31 us (30%)
  waiting for transfers between devices  12.9 us (12%)
  Pallas kernels  7.64 us (7%)
  between operations  2.02 us (2%)
    all_to_all x3, blocking collectives, exchange(): return lax.all_to_all(chunks, axis, 0, 0, tiled=True)  49.9 us
    all_to_all x1, starting transfers between devices, exchange(): return lax.all_to_all(chunks, axis, 0, 0, tiled=True)  23.7 us
    all_to_all x1, waiting for transfers between devices, exchange(): return lax.all_to_all(chunks, axis, 0, 0, tiled=True)  12.9 us
    ppermute x2, starting transfers between devices, partner(): lax.ppermute(block, 'col', [(k, k ^ count // 2) for k in range(count)])  7.33 us
  transfers between devices with their start and end apart: 3, of which 1 were waited for; matrix products, arithmetic and copies ran while one was open for 1% of the time, Pallas kernels for 4%

profile of v6, /device:TPU:72, one launch (start us, length us, event | category | flops | bytes accessed | tf_op | source)
XLA Modules:
  0.0 104.3 jit_solution(18349136525118145286)
XLA Ops:
  0.6 4.9 %collective-permute-start.1 = (bf16[8,256,256]{2,1,0:T(8,128)(2,1)}, bf16[8,256,256]{2,1,0:T(8,128)(2,1)S(1)}, u32[]{:S(2)}, u32[]{:S(2)}) collective-permute-start(bf16[8,256,256]{2,1,0:T(8,128)(2,1)} %bitcast.21), channel_id=1, source_target_pairs={{0,16},{1,17},{2,18},{3,19},{4,20},{5,21},{6,22},{7,23},{8,24},{9,... | collective-permute-start | bytes 3145736 | tf_op jit(solution)/shard_map/ppermute | solution.py:268
  5.6 1.5 %shard_map.122 = bf16[32,16,128]{2,1,0:T(8,128)(2,1)} custom-call(bf16[32,64]{1,0:T(8,128)(2,1)} %bitcast.18, f32[16,128]{1,0:T(8,128)} %bitcast.13), custom_call_target="tpu_custom_call" | custom-call | tf_op jit(solution)/shard_map/pallas_call | solution.py:303
  7.0 23.7 %all-to-all-start = ((bf16[32,16,128]{2,1,0:T(8,128)(2,1)}), bf16[32,16,128]{2,1,0:T(8,128)(2,1)S(1)}, u32[]{:S(2)}, u32[]{:S(2)}) async-start(bf16[32,16,128]{2,1,0:T(8,128)(2,1)} %shard_map.122), calls=%async_computation | async-start | bytes 262144 | tf_op jit(solution)/shard_map/all_to_all | solution.py:263
  31.4 0.1 pad.2.clone
  31.4 0.7 add_add_fusion
  32.2 2.4 %collective-permute-start = (s32[3,8]{1,0:T(4,128)S(1)}, s32[3,8]{1,0:T(4,128)S(1)}, u32[]{:S(2)}, u32[]{:S(2)}) collective-permute-start(s32[3,8]{1,0:T(4,128)S(1)} %add_add_fusion), channel_id=1, source_target_pairs={{0,16},{1,17},{2,18},{3,19},{4,20},{5,21},{6,22},{7,23},{8,24},{9,... | collective-permute-start | bytes 296 | tf_op jit(solution)/shard_map/ppermute | solution.py:268
  35.2 1.5 %shard_map.123.tiles_ref = bf16[16,256,256]{2,1,0:T(8,128)(2,1)S(1)} custom-call(s32[1,1]{1,0:T(1,128)S(6)} %copy.13.count_ref, bf16[16,256,256]{2,1,0:T(8,128)(2,1)} %bitcast.16), custom_call_target="tpu_custom_call" | custom-call | tf_op jit(solution)/shard_map/pallas_call | solution.py:227
  36.7 0.0 copy-start.1
  36.7 12.9 %all-to-all-done.source_ref = bf16[32,16,128]{2,1,0:T(8,128)(2,1)S(1)} async-done(((bf16[32,16,128]{2,1,0:T(8,128)(2,1)}), bf16[32,16,128]{2,1,0:T(8,128)(2,1)S(1)}, u32[]{:S(2)}, u32[]{:S(2)}) %all-to-all-start) | async-done | bytes 131104 | tf_op jit(solution)/shard_map/all_to_all | solution.py:263
  49.7 1.6 %shard_map.124 = (f32[8,32,256]{2,1,0:T(8,128)S(1)}, bf16[8,32,256]{2,1,0:T(8,128)(2,1)S(1)}) custom-call(s32[1,1,16]{2,1,0:T(1,128)} %rows_ref.3, s32[1,1,16]{2,1,0:T(1,128)} %cols_ref.3, s32[1,1]{1,0:T(1,128)S(6)} %copy.13.count_ref, bf16[32,16,128]{2,1,0:T(8,128)(2,1)S(1)} %all-to-all-done.source_ref, bf16[16,256,256]{2,1,0:T(8,128)(2,1)S(1)} %shard_map.123.tiles_ref), custom_call_target="tpu_custom_call" | custom-call | tf_op jit(solution)/shard_map/pallas_call | solution.py:131
  51.3 0.0 collective-permute-done.index_ref
  51.3 0.0 collective-permute-done.1.home_ref
  51.3 0.7 shard_map.125
  52.0 0.0 copy-start
  52.0 12.1 %all_to_all.20.received_ref = bf16[32,16,128]{2,1,0:T(8,128)(2,1)S(1)} all-to-all(bf16[32,16,128]{2,1,0:T(8,128)(2,1)S(1)} %shard_map.125), channel_id=1, replica_groups=mesh['row'=32,'col'=32] {'col'}, dimensions={0} | all-to-all | bytes 262144 | tf_op jit(solution)/shard_map/all_to_all | solution.py:263
  64.1 0.0 copy-done.1
  64.1 0.2 shard_map.126
  64.3 12.1 %all_to_all.21.source_ref = bf16[32,16,128]{2,1,0:T(8,128)(2,1)S(1)} all-to-all(bf16[32,16,128]{2,1,0:T(8,128)(2,1)S(1)} %get-tuple-element.10), channel_id=1, replica_groups=mesh['row'=32,'col'=32] {'col'}, dimensions={0} | all-to-all | bytes 262144 | tf_op jit(solution)/shard_map/all_to_all | solution.py:263
  76.3 1.5 %shard_map.127 = (bf16[32,16,128]{2,1,0:T(8,128)(2,1)S(1)}, f32[32,64]{1,0:T(8,128)}) custom-call(s32[1,1,16]{2,1,0:T(1,128)} %rows_ref.3, s32[1,1,16]{2,1,0:T(1,128)} %cols_ref.3, s32[1,1]{1,0:T(1,128)S(6)} %copy.13.count_ref, s32[3,8]{1,0:T(4,128)S(1)} %collective-permute-done.index_ref, bf16[32,16,128]{2,1,0:T(8,128)(2,1)S(1)} %all_to_all.21.source_ref, ...), custom_call_target="tpu_custom_call" | custom-call | tf_op jit(solution)/shard_map/pallas_call | solution.py:191
  77.8 25.8 %all_to_all.22.received_ref = bf16[32,16,128]{2,1,0:T(8,128)(2,1)S(1)} all-to-all(bf16[32,16,128]{2,1,0:T(8,128)(2,1)S(1)} %get-tuple-element.13), channel_id=1, replica_groups=mesh['row'=32,'col'=32] {'row'}, dimensions={0} | all-to-all | bytes 262144 | tf_op jit(solution)/shard_map/all_to_all | solution.py:263
  103.6 0.0 copy-done
  103.6 0.8 shard_map.128
Async XLA Ops:
  0.6 50.7 %collective-permute-start.1 = (bf16[8,256,256]{2,1,0:T(8,128)(2,1)}, bf16[8,256,256]{2,1,0:T(8,128)(2,1)S(1)}, u32[]{:S(2)}, u32[]{:S(2)}) collective-permute-start(bf16[8,256,256]{2,1,0:T(8,128)(2,1)} %bitcast.21), channel_id=1, source_target_pairs={{0,16},{1,17},{2,18},{3,19},{4,20},{5,21},{6,22},{7,23},{8,24},{9,... | collective-permute-start | bytes 3145736 | tf_op jit(solution)/shard_map/ppermute | solution.py:268
  7.0 42.6 %all-to-all-start = ((bf16[32,16,128]{2,1,0:T(8,128)(2,1)}), bf16[32,16,128]{2,1,0:T(8,128)(2,1)S(1)}, u32[]{:S(2)}, u32[]{:S(2)}) async-start(bf16[32,16,128]{2,1,0:T(8,128)(2,1)} %shard_map.122), calls=%async_computation | async-start | bytes 262144 | tf_op jit(solution)/shard_map/all_to_all | solution.py:263
  32.2 19.1 %collective-permute-start = (s32[3,8]{1,0:T(4,128)S(1)}, s32[3,8]{1,0:T(4,128)S(1)}, u32[]{:S(2)}, u32[]{:S(2)}) collective-permute-start(s32[3,8]{1,0:T(4,128)S(1)} %add_add_fusion), channel_id=1, source_target_pairs={{0,16},{1,17},{2,18},{3,19},{4,20},{5,21},{6,22},{7,23},{8,24},{9,... | collective-permute-start | bytes 296 | tf_op jit(solution)/shard_map/ppermute | solution.py:268
  36.7 27.4 %copy-start.1 = (f32[2048]{0:T(1024)S(1)}, f32[2048]{0:T(1024)}, u32[]{:S(2)}) copy-start(f32[2048]{0:T(1024)} %param.12) | copy-start | bytes 24580
  52.0 51.6 %copy-start = (f32[2048]{0:T(1024)S(1)}, f32[2048]{0:T(1024)}, u32[]{:S(2)}) copy-start(f32[2048]{0:T(1024)} %param.13) | copy-start | bytes 24580

commit v7 on v5

--- a/solution.py
+++ b/solution.py
@@ -5,7 +5,6 @@
 from jax.experimental.pallas import tpu as pltpu
 from jax.sharding import PartitionSpec as P
 
-GROUP = 8
 SMALL = pltpu.CompilerParams(vmem_limit_bytes=4 * 1024 * 1024)
 F32 = jnp.float32
 BF16 = jnp.bfloat16
@@ -86,21 +85,14 @@
 def add_tiles(in_at, out_at, used, wide_ref, total_ref, tiles_ref, flip):
     contract = (((1,), (0,)), ((), ())) if flip else (((1,), (1,)), ((), ()))
 
-    def body(group, carry):
-        base = group * GROUP
-        prods = []
-        for step in range(GROUP):
-            slot = base + step
+    @pl.when(used > 0)
+    def _():
+        for slot in range(tiles_ref.shape[0]):
             prod = lax.dot_general(
                 wide_ref[in_at(slot)], tiles_ref[slot], contract, preferred_element_type=F32
             )
-            prods.append(jnp.where(slot < used, prod, 0.0))
-        for step in range(GROUP):
-            spot = out_at(base + step)
-            total_ref[spot] = total_ref[spot] + prods[step]
-        return carry
-
-    lax.fori_loop(0, (used + GROUP - 1) // GROUP, body, 0)
+            spot = out_at(slot)
+            total_ref[spot] = total_ref[spot] + jnp.where(slot < used, prod, 0.0)
 
 
 def product_kernel(flip, carried):

time: 104 us -> 105 us (level)
  no operation moved by 1% of the time
where the time goes in v7:
time: 105 us; the launch traced here: 104 us
  blocking collectives  50 us (48%)
  starting transfers between devices  31 us (30%)
  waiting for transfers between devices  14.6 us (14%)
  Pallas kernels  6.58 us (6%)
  between operations  1.99 us (2%)
    all_to_all x3, blocking collectives, exchange(): return lax.all_to_all(chunks, axis, 0, 0, tiled=True)  50 us
    all_to_all x1, starting transfers between devices, exchange(): return lax.all_to_all(chunks, axis, 0, 0, tiled=True)  23.7 us
    all_to_all x1, waiting for transfers between devices, exchange(): return lax.all_to_all(chunks, axis, 0, 0, tiled=True)  11.9 us
    ppermute x2, starting transfers between devices, partner(): lax.ppermute(block, 'col', [(k, k ^ count // 2) for k in range(count)])  7.35 us
    pallas_call x2, Pallas kernels, product(): pl.pallas_call(product_kernel(flip, kept is not None), compiler_params=SM...  2.96 us
    ppermute x2, waiting for transfers between devices, partner(): lax.ppermute(block, 'col', [(k, k ^ count // 2) for k in range(count)])  2.65 us
  transfers between devices with their start and end apart: 3, of which 2 were waited for; matrix products, arithmetic and copies ran while one was open for 0% of the time, Pallas kernels for 3%

profile of v7, /device:TPU:72, one launch (start us, length us, event | category | flops | bytes accessed | tf_op | source)
XLA Modules:
  0.0 104.2 jit_solution(4188587273597078575)
XLA Ops:
  0.6 4.9 %collective-permute-start.1 = (bf16[8,256,256]{2,1,0:T(8,128)(2,1)}, bf16[8,256,256]{2,1,0:T(8,128)(2,1)S(1)}, u32[]{:S(2)}, u32[]{:S(2)}) collective-permute-start(bf16[8,256,256]{2,1,0:T(8,128)(2,1)} %bitcast.13), channel_id=1, source_target_pairs={{0,16},{1,17},{2,18},{3,19},{4,20},{5,21},{6,22},{7,23},{8,24},{9,... | collective-permute-start | bytes 3145736 | tf_op jit(solution)/shard_map/ppermute | solution.py:206
  6.2 1.5 %shard_map.122 = (bf16[32,16,128]{2,1,0:T(8,128)(2,1)}, s32[3,8]{1,0:T(4,128)S(1)}) custom-call(bf16[32,64]{1,0:T(8,128)(2,1)} %bitcast.12, f32[16,128]{1,0:T(8,128)} %bitcast.7, s32[1,1,8]{2,1,0:T(1,128)} %lent_rows_ref.1, s32[1,1,8]{2,1,0:T(1,128)} %lent_cols_ref.1, s32[1,1]{1,0:T(1,128)S(6)} %copy.14.lent_count_ref), custom_call_target="tpu_custom_call" | custom-call | tf_op jit(solution)/shard_map/pallas_call | solution.py:233
  7.7 23.7 %all-to-all-start = ((bf16[32,16,128]{2,1,0:T(8,128)(2,1)}), bf16[32,16,128]{2,1,0:T(8,128)(2,1)S(1)}, u32[]{:S(2)}, u32[]{:S(2)}) async-start(bf16[32,16,128]{2,1,0:T(8,128)(2,1)} %get-tuple-element.9), calls=%async_computation | async-start | bytes 262144 | tf_op jit(solution)/shard_map/all_to_all | solution.py:201
  31.4 2.4 %collective-permute-start = (s32[3,8]{1,0:T(4,128)S(1)}, s32[3,8]{1,0:T(4,128)S(1)}, u32[]{:S(2)}, u32[]{:S(2)}) collective-permute-start(s32[3,8]{1,0:T(4,128)S(1)} %get-tuple-element.8), channel_id=1, source_target_pairs={{0,16},{1,17},{2,18},{3,19},{4,20},{5,21},{6,22},{7,23},{8,24},{9,... | collective-permute-start | bytes 296 | tf_op jit(solution)/shard_map/ppermute | solution.py:206
  34.4 1.2 %shard_map.123.refs_5_ = bf16[16,256,256]{2,1,0:T(8,128)(2,1)S(1)} custom-call(s32[1,1]{1,0:T(1,128)S(6)} %copy.13.count_ref.refs_2_, bf16[16,256,256]{2,1,0:T(8,128)(2,1)} %bitcast.10), custom_call_target="tpu_custom_call" | custom-call | tf_op jit(solution)/shard_map/pallas_call | solution.py:165
  35.7 0.0 copy-start.1
  35.7 2.6 %collective-permute-done.refs_3_ = s32[3,8]{1,0:T(4,128)S(1)} collective-permute-done((s32[3,8]{1,0:T(4,128)S(1)}, s32[3,8]{1,0:T(4,128)S(1)}, u32[]{:S(2)}, u32[]{:S(2)}) %collective-permute-start) | collective-permute-done | bytes 128 | tf_op jit(solution)/shard_map/ppermute | solution.py:206
  38.4 11.9 %all-to-all-done.refs_4_ = bf16[32,16,128]{2,1,0:T(8,128)(2,1)S(1)} async-done(((bf16[32,16,128]{2,1,0:T(8,128)(2,1)}), bf16[32,16,128]{2,1,0:T(8,128)(2,1)S(1)}, u32[]{:S(2)}, u32[]{:S(2)}) %all-to-all-start) | async-done | bytes 131104 | tf_op jit(solution)/shard_map/all_to_all | solution.py:201
  50.3 0.0 collective-permute-done.1.refs_6_
  50.3 1.6 %shard_map.124 = bf16[32,16,128]{2,1,0:T(8,128)(2,1)S(1)} custom-call(s32[1,1,16]{2,1,0:T(1,128)} %refs_0_.3, s32[1,1,16]{2,1,0:T(1,128)} %refs_1_.3, s32[1,1]{1,0:T(1,128)S(6)} %copy.13.count_ref.refs_2_, s32[3,8]{1,0:T(4,128)S(1)} %collective-permute-done.refs_3_, bf16[32,16,128]{2,1,0:T(8,128)(2,1)S(1)} %all-to-all-done.refs_4_, ...), custom_call_target="tpu_custom_call" | custom-call | tf_op jit(solution)/shard_map/pallas_call | solution.py:136
  51.9 0.0 copy-start
  51.9 12.5 %all_to_all.20.received_ref = bf16[32,16,128]{2,1,0:T(8,128)(2,1)S(1)} all-to-all(bf16[32,16,128]{2,1,0:T(8,128)(2,1)S(1)} %shard_map.124), channel_id=1, replica_groups=mesh['row'=32,'col'=32] {'col'}, dimensions={0} | all-to-all | bytes 262144 | tf_op jit(solution)/shard_map/all_to_all | solution.py:201
  64.4 0.0 copy-done.1
  64.5 0.2 shard_map.125
  64.6 12.1 %all_to_all.21.refs_4_ = bf16[32,16,128]{2,1,0:T(8,128)(2,1)S(1)} all-to-all(bf16[32,16,128]{2,1,0:T(8,128)(2,1)S(1)} %get-tuple-element.10), channel_id=1, replica_groups=mesh['row'=32,'col'=32] {'col'}, dimensions={0} | all-to-all | bytes 262144 | tf_op jit(solution)/shard_map/all_to_all | solution.py:201
  76.7 1.4 %shard_map.126 = (bf16[32,16,128]{2,1,0:T(8,128)(2,1)S(1)}, f32[32,64]{1,0:T(8,128)}) custom-call(s32[1,1,16]{2,1,0:T(1,128)} %refs_0_.3, s32[1,1,16]{2,1,0:T(1,128)} %refs_1_.3, s32[1,1]{1,0:T(1,128)S(6)} %copy.13.count_ref.refs_2_, s32[3,8]{1,0:T(4,128)S(1)} %collective-permute-done.refs_3_, bf16[32,16,128]{2,1,0:T(8,128)(2,1)S(1)} %all_to_all.21.refs_4_, ...), custom_call_target="tpu_custom_call" | custom-call | tf_op jit(solution)/shard_map/pallas_call | solution.py:136
  78.0 25.4 %all_to_all.22.received_ref = bf16[32,16,128]{2,1,0:T(8,128)(2,1)S(1)} all-to-all(bf16[32,16,128]{2,1,0:T(8,128)(2,1)S(1)} %get-tuple-element.13), channel_id=1, replica_groups=mesh['row'=32,'col'=32] {'row'}, dimensions={0} | all-to-all | bytes 262144 | tf_op jit(solution)/shard_map/all_to_all | solution.py:201
  103.4 0.0 copy-done
  103.4 0.8 shard_map.127
Async XLA Ops:
  0.6 49.7 %collective-permute-start.1 = (bf16[8,256,256]{2,1,0:T(8,128)(2,1)}, bf16[8,256,256]{2,1,0:T(8,128)(2,1)S(1)}, u32[]{:S(2)}, u32[]{:S(2)}) collective-permute-start(bf16[8,256,256]{2,1,0:T(8,128)(2,1)} %bitcast.13), channel_id=1, source_target_pairs={{0,16},{1,17},{2,18},{3,19},{4,20},{5,21},{6,22},{7,23},{8,24},{9,... | collective-permute-start | bytes 3145736 | tf_op jit(solution)/shard_map/ppermute | solution.py:206
  7.7 42.6 %all-to-all-start = ((bf16[32,16,128]{2,1,0:T(8,128)(2,1)}), bf16[32,16,128]{2,1,0:T(8,128)(2,1)S(1)}, u32[]{:S(2)}, u32[]{:S(2)}) async-start(bf16[32,16,128]{2,1,0:T(8,128)(2,1)} %get-tuple-element.9), calls=%async_computation | async-start | bytes 262144 | tf_op jit(solution)/shard_map/all_to_all | solution.py:201
  31.4 7.0 %collective-permute-start = (s32[3,8]{1,0:T(4,128)S(1)}, s32[3,8]{1,0:T(4,128)S(1)}, u32[]{:S(2)}, u32[]{:S(2)}) collective-permute-start(s32[3,8]{1,0:T(4,128)S(1)} %get-tuple-element.8), channel_id=1, source_target_pairs={{0,16},{1,17},{2,18},{3,19},{4,20},{5,21},{6,22},{7,23},{8,24},{9,... | collective-permute-start | bytes 296 | tf_op jit(solution)/shard_map/ppermute | solution.py:206
  35.7 28.8 %copy-start.1 = (f32[2048]{0:T(1024)S(1)}, f32[2048]{0:T(1024)}, u32[]{:S(2)}) copy-start(f32[2048]{0:T(1024)} %param.12) | copy-start | bytes 24580
  51.9 51.5 %copy-start = (f32[2048]{0:T(1024)S(1)}, f32[2048]{0:T(1024)}, u32[]{:S(2)}) copy-start(f32[2048]{0:T(1024)} %param.13) | copy-start | bytes 24580
